TPU v7x, 32 devices: a whole 2x2x4 slice. The times are simulated.
32 devices in a mesh: gx: 4 (over y, x), gy: 8 (over z, core).
Axes of the slice: x: 2, y: 2, z: 4, core: 2. Of those that a mesh axis runs over, the one named last changes fastest.
Arguments:
- potential: float32 [96, 128, 128], P('gx', 'gy'), may hold values from -0.875 to 0.875
- density: float32 [96, 128, 128], P('gx', 'gy'), may hold values from 0.5 to 2
- correction: float32 [96, 128, 128], P('gx', 'gy'), may hold values from -6 to 6
Outputs:
- updated: float32 [96, 128, 128], P('gx', 'gy')
- residual: float32 [96, 128, 128], P('gx', 'gy')
All inputs are finite; a program needn't handle non-finite values.
Results may differ from a plain program's by a relative error of at most 0.0003.
Values sent between devices are 32-bit elements; how exact they have to be, the bound alone decides.
A program may use at most 64 MiB of HBM per device.

v0:
```python
import jax
import jax.numpy as jnp
from jax import lax
from jax.sharding import PartitionSpec as P

FACTOR = 4
PRE = 2
POST = 2
COARSE_SWEEPS = 4


screening = 0.002
damping = 0.6


def extended_2(cells, sides, width):
    for axis, dim in sides:
        count = lax.axis_size(axis)
        head = lax.slice_in_dim(cells, 0, width, axis=dim)
        tail = lax.slice_in_dim(cells, cells.shape[dim] - width, cells.shape[dim], axis=dim)
        cells = jnp.concatenate(
            [
                lax.ppermute(tail, axis, [(i, (i + 1) % count) for i in range(count)]),
                cells,
                lax.ppermute(head, axis, [((i + 1) % count, i) for i in range(count)]),
            ],
            axis=dim,
        )
    return cells


def cropper(values):
    inner_x = values.shape[0] - 2
    inner_y = values.shape[1] - 2

    def getter(shift_x, shift_y, shift_z):
        window = values[1 + shift_x : 1 + shift_x + inner_x, 1 + shift_y : 1 + shift_y + inner_y, :]
        if shift_z:
            return jnp.roll(window, -shift_z, axis=2)
        return window

    return getter


def shrink(values, margin):
    return values[margin : values.shape[0] - margin, margin : values.shape[1] - margin, :]


def hessian(getter):
    centre = getter(0, 0, 0)

    def second(shift_x, shift_y, shift_z):
        return (
            getter(shift_x, shift_y, shift_z) + getter(-shift_x, -shift_y, -shift_z) - 2.0 * centre
        )

    def cross_term(ax_x, ax_y, ax_z, bx_x, bx_y, bx_z):
        plus_plus = getter(ax_x + bx_x, ax_y + bx_y, ax_z + bx_z)
        plus_minus = getter(ax_x - bx_x, ax_y - bx_y, ax_z - bx_z)
        minus_plus = getter(bx_x - ax_x, bx_y - ax_y, bx_z - ax_z)
        minus_minus = getter(-ax_x - bx_x, -ax_y - bx_y, -ax_z - bx_z)
        return 0.25 * (plus_plus - plus_minus - minus_plus + minus_minus)

    return (
        second(1, 0, 0),
        second(0, 1, 0),
        second(0, 0, 1),
        cross_term(1, 0, 0, 0, 1, 0),
        cross_term(1, 0, 0, 0, 0, 1),
        cross_term(0, 1, 0, 0, 0, 1),
    )


def cofactors(hess):
    mat_xx = 1.0 + hess[0]
    mat_yy = 1.0 + hess[1]
    mat_zz = 1.0 + hess[2]
    mat_xy, mat_xz, mat_yz = (hess[3], hess[4], hess[5])
    cof_xx = mat_yy * mat_zz - mat_yz * mat_yz
    cof_yy = mat_xx * mat_zz - mat_xz * mat_xz
    cof_zz = mat_xx * mat_yy - mat_xy * mat_xy
    cof_xy = mat_xz * mat_yz - mat_xy * mat_zz
    cof_xz = mat_xy * mat_yz - mat_xz * mat_yy
    cof_yz = mat_xy * mat_xz - mat_xx * mat_yz
    determinant = mat_xx * cof_xx + mat_xy * cof_xy + mat_xz * cof_xz
    return ((cof_xx, cof_yy, cof_zz, cof_xy, cof_xz, cof_yz), determinant)


def operate(getter, coeffs, spacing):
    centre = getter(0, 0, 0)
    terms = hessian(getter)
    summed = coeffs[0] * terms[0] + coeffs[1] * terms[1] + coeffs[2] * terms[2]
    summed = summed + 2.0 * (coeffs[3] * terms[3] + coeffs[4] * terms[4] + coeffs[5] * terms[5])
    return spacing * summed - screening * centre


def diagonal_of(coeffs, spacing):
    return -2.0 * spacing * (coeffs[0] + coeffs[1] + coeffs[2]) - screening


def relax_padded(padded, coeffs, diagonal, source, spacing):
    centre = shrink(padded, 1)
    return centre + damping * (source - operate(cropper(padded), coeffs, spacing)) / diagonal


def rim_one(values):
    return extended_2(values, (("gx", 0), ("gy", 1)), 1)


def pool_table(length):
    rows_idx = jnp.arange(length)[:, None] // FACTOR
    cols_idx = jnp.arange(length // FACTOR)[None, :]
    return (rows_idx == cols_idx).astype(jnp.float32)


def block_mean(values, table):
    size_x, size_y, size_z = values.shape
    pooled = (
        jnp.dot(values.reshape(size_x * size_y, size_z), table, precision=lax.Precision.HIGHEST)
        / FACTOR
    )
    pooled = pooled.reshape(size_x // FACTOR, FACTOR, size_y // FACTOR, FACTOR, size_z // FACTOR)
    return jnp.mean(pooled, axis=(1, 3))


def spread_up(values, table):
    size_x, size_y, size_z = values.shape
    grown_z = jnp.dot(
        values.reshape(size_x * size_y, size_z), table.T, precision=lax.Precision.HIGHEST
    )
    grown_z = grown_z.reshape(size_x, 1, size_y, 1, size_z * FACTOR)
    grown = jnp.broadcast_to(grown_z, (size_x, FACTOR, size_y, FACTOR, size_z * FACTOR))
    return grown.reshape(size_x * FACTOR, size_y * FACTOR, size_z * FACTOR)


def shards(potential, density, correction):
    padded = extended_2(potential, (("gx", 0), ("gy", 1)), 1)
    coeffs, determinant = cofactors(hessian(cropper(padded)))
    source = density - determinant
    diagonal = diagonal_of(coeffs, 1.0)

    def smooth(estimate, count):
        for counter in range(count):
            estimate = relax_padded(rim_one(estimate), coeffs, diagonal, source, 1.0)
        return estimate

    estimate = smooth(correction, PRE)
    fine_residual = source - operate(cropper(rim_one(estimate)), coeffs, 1.0)
    table = pool_table(fine_residual.shape[2])
    coarse_source = block_mean(fine_residual, table)
    coarse_coeffs = tuple((block_mean(entry, table) for entry in coeffs))
    coarse_spacing = 1.0 / FACTOR**2
    coarse_diagonal = diagonal_of(coarse_coeffs, coarse_spacing)
    coarse = damping * coarse_source / coarse_diagonal
    for counter in range(COARSE_SWEEPS - 1):
        extended = extended_2(coarse, (("gx", 0), ("gy", 1)), 1)
        coarse = relax_padded(
            extended, coarse_coeffs, coarse_diagonal, coarse_source, coarse_spacing
        )
    estimate = estimate + spread_up(coarse, table)
    estimate = smooth(estimate, POST)
    residual = source - operate(cropper(rim_one(estimate)), coeffs, 1.0)
    return (estimate, residual)


def solution(mesh):
    placed = (P("gx", "gy", None), P("gx", "gy", None), P("gx", "gy", None))
    return jax.shard_map(
        shards,
        mesh=mesh,
        in_specs=placed,
        out_specs=(P("gx", "gy", None), P("gx", "gy", None)),
        check_vma=False,
    )
```

profile of v0, /device:TPU:0, one launch (start us, length us, event | category | flops | bytes accessed | tf_op | source)
XLA Modules:
  0.0 118.1 jit_solution(14542648108687611334)
XLA Ops:
  1.3 2.9 %collective-permute-start.1 = (f32[1,16,128]{2,1,0:T(8,128)S(1)}, f32[1,16,128]{2,1,0:T(8,128)S(1)}, u32[]{:S(2)}, u32[]{:S(2)}) collective-permute-start(f32[1,16,128]{2,1,0:T(8,128)S(1)} %get-tuple-element.192), channel_id=1, source_target_pairs={{0,8},{8,16},{16,24},{24,0},{1,9},{9,17},{17,25},{25,1},{2,10},{10... | collective-permute-start | bytes 24584 | tf_op jit(solution)/shard_map/ppermute | solution.py:23
  7.0 1.9 %collective-permute-start.4 = (f32[1,16,128]{2,1,0:T(8,128)S(1)}, f32[1,16,128]{2,1,0:T(8,128)S(1)}, u32[]{:S(2)}, u32[]{:S(2)}) collective-permute-start(f32[1,16,128]{2,1,0:T(8,128)S(1)} %get-tuple-element.200), channel_id=1, source_target_pairs={{8,0},{16,8},{24,16},{0,24},{9,1},{17,9},{25,17},{1,25},{10,2},{18... | collective-permute-start | bytes 24584 | tf_op jit(solution)/shard_map/ppermute | solution.py:25
  12.4 2.4 %collective-permute-start.2 = (f32[26,1,128]{2,1,0:T(1,128)S(1)}, f32[26,1,128]{2,1,0:T(1,128)S(1)}, u32[]{:S(2)}, u32[]{:S(2)}) collective-permute-start(f32[26,1,128]{2,1,0:T(1,128)S(1)} %get-tuple-element.88), channel_id=1, source_target_pairs={{1,0},{2,1},{3,2},{4,3},{5,4},{6,5},{7,6},{0,7},{9,8},{10,9},{11,1... | collective-permute-start | bytes 39944 | tf_op jit(solution)/shard_map/ppermute | solution.py:25
  14.9 3.6 %collective-permute-start.6 = (f32[26,1,128]{2,1,0:T(1,128)S(1)}, f32[26,1,128]{2,1,0:T(1,128)S(1)}, u32[]{:S(2)}, u32[]{:S(2)}) collective-permute-start(f32[26,1,128]{2,1,0:T(1,128)S(1)} %get-tuple-element.94), channel_id=1, source_target_pairs={{1,0},{2,1},{3,2},{4,3},{5,4},{6,5},{7,6},{0,7},{9,8},{10,9},{11,1... | collective-permute-start | bytes 39944 | tf_op jit(solution)/shard_map/ppermute | solution.py:25
  18.5 1.3 %collective-permute-done.3 = f32[26,1,128]{2,1,0:T(1,128)S(1)} collective-permute-done((f32[26,1,128]{2,1,0:T(1,128)S(1)}, f32[26,1,128]{2,1,0:T(1,128)S(1)}, u32[]{:S(2)}, u32[]{:S(2)}) %collective-permute-start.3) | collective-permute-done | bytes 13344 | tf_op jit(solution)/shard_map/ppermute | solution.py:23
  20.2 3.2 %collective-permute-done.7 = f32[26,1,128]{2,1,0:T(1,128)S(1)} collective-permute-done((f32[26,1,128]{2,1,0:T(1,128)S(1)}, f32[26,1,128]{2,1,0:T(1,128)S(1)}, u32[]{:S(2)}, u32[]{:S(2)}) %collective-permute-start.7) | collective-permute-done | bytes 13344 | tf_op jit(solution)/shard_map/ppermute | solution.py:23
  24.8 1.3 %fusion.101 = (f32[24,16,128]{2,1,0:T(8,128)S(1)}, f32[24,16,128]{2,1,0:T(8,128)S(1)}, f32[24,16,128]{2,1,0:T(8,128)S(1)}, f32[24,16,128]{2,1,0:T(8,128)S(1)}, f...) fusion(f32[24,16,128]{2,1,0:T(8,128)S(1)} %copy-done.2, ...), kind=kLoop, calls=%fused_computation.206 | loop fusion | flops 4866048 | bytes 6534144 | tf_op jit(solution)/shard_map/add | solution.py:103
  29.8 1.8 %collective-permute-done.9 = f32[1,16,128]{2,1,0:T(8,128)S(1)} collective-permute-done((f32[1,16,128]{2,1,0:T(8,128)S(1)}, f32[1,16,128]{2,1,0:T(8,128)S(1)}, u32[]{:S(2)}, u32[]{:S(2)}) %collective-permute-start.9) | collective-permute-done | bytes 8224 | tf_op jit(solution)/shard_map/ppermute | solution.py:23
  33.1 3.6 %collective-permute-done.11 = f32[26,1,128]{2,1,0:T(1,128)S(1)} collective-permute-done((f32[26,1,128]{2,1,0:T(1,128)S(1)}, f32[26,1,128]{2,1,0:T(1,128)S(1)}, u32[]{:S(2)}, u32[]{:S(2)}) %collective-permute-start.11) | collective-permute-done | bytes 13344 | tf_op jit(solution)/shard_map/ppermute | solution.py:23
  37.8 1.2 %collective-permute-start.12 = (f32[1,16,128]{2,1,0:T(8,128)S(1)}, f32[1,16,128]{2,1,0:T(8,128)S(1)}, u32[]{:S(2)}, u32[]{:S(2)}) collective-permute-start(f32[1,16,128]{2,1,0:T(8,128)S(1)} %get-tuple-element.170), channel_id=1, source_target_pairs={{8,0},{16,8},{24,16},{0,24},{9,1},{17,9},{25,17},{1,25},{10,2},{18... | collective-permute-start | bytes 24584 | tf_op jit(solution)/shard_map/ppermute | solution.py:25
  41.5 2.0 %collective-permute-done.13 = f32[1,16,128]{2,1,0:T(8,128)S(1)} collective-permute-done((f32[1,16,128]{2,1,0:T(8,128)S(1)}, f32[1,16,128]{2,1,0:T(8,128)S(1)}, u32[]{:S(2)}, u32[]{:S(2)}) %collective-permute-start.13) | collective-permute-done | bytes 8224 | tf_op jit(solution)/shard_map/ppermute | solution.py:23
  45.1 3.6 %collective-permute-done.15 = f32[26,1,128]{2,1,0:T(1,128)S(1)} collective-permute-done((f32[26,1,128]{2,1,0:T(1,128)S(1)}, f32[26,1,128]{2,1,0:T(1,128)S(1)}, u32[]{:S(2)}, u32[]{:S(2)}) %collective-permute-start.15) | collective-permute-done | bytes 13344 | tf_op jit(solution)/shard_map/ppermute | solution.py:23
  53.9 1.8 %collective-permute-done.17 = f32[1,4,32]{2,1,0:T(4,128)S(1)} collective-permute-done((f32[1,4,32]{2,1,0:T(4,128)S(1)}, f32[1,4,32]{2,1,0:T(4,128)S(1)}, u32[]{:S(2)}, u32[]{:S(2)}) %collective-permute-start.17) | collective-permute-done | bytes 544 | tf_op jit(solution)/shard_map/ppermute | solution.py:23
  57.2 3.6 %collective-permute-done.19 = f32[8,1,32]{2,1,0:T(1,128)S(1)} collective-permute-done((f32[8,1,32]{2,1,0:T(1,128)S(1)}, f32[8,1,32]{2,1,0:T(1,128)S(1)}, u32[]{:S(2)}, u32[]{:S(2)}) %collective-permute-start.19) | collective-permute-done | bytes 1056 | tf_op jit(solution)/shard_map/ppermute | solution.py:23
  61.4 1.9 %collective-permute-start.21 = (f32[1,4,32]{2,1,0:T(4,128)S(1)}, f32[1,4,32]{2,1,0:T(4,128)S(1)}, u32[]{:S(2)}, u32[]{:S(2)}) collective-permute-start(f32[1,4,32]{2,1,0:T(4,128)S(1)} %get-tuple-element.270), channel_id=1, source_target_pairs={{0,8},{8,16},{16,24},{24,0},{1,9},{9,17},{17,25},{25,1},{2,10},{10... | collective-permute-start | bytes 1544 | tf_op jit(solution)/shard_map/ppermute | solution.py:23
  63.3 1.6 %collective-permute-done.20 = f32[1,4,32]{2,1,0:T(4,128)S(1)} collective-permute-done((f32[1,4,32]{2,1,0:T(4,128)S(1)}, f32[1,4,32]{2,1,0:T(4,128)S(1)}, u32[]{:S(2)}, u32[]{:S(2)}) %collective-permute-start.20) | collective-permute-done | bytes 544 | tf_op jit(solution)/shard_map/ppermute | solution.py:25
  67.3 3.6 %collective-permute-done.23 = f32[8,1,32]{2,1,0:T(1,128)S(1)} collective-permute-done((f32[8,1,32]{2,1,0:T(1,128)S(1)}, f32[8,1,32]{2,1,0:T(1,128)S(1)}, u32[]{:S(2)}, u32[]{:S(2)}) %collective-permute-start.23) | collective-permute-done | bytes 1056 | tf_op jit(solution)/shard_map/ppermute | solution.py:23
  73.4 1.6 %collective-permute-done.24 = f32[1,4,32]{2,1,0:T(4,128)S(1)} collective-permute-done((f32[1,4,32]{2,1,0:T(4,128)S(1)}, f32[1,4,32]{2,1,0:T(4,128)S(1)}, u32[]{:S(2)}, u32[]{:S(2)}) %collective-permute-start.24) | collective-permute-done | bytes 544 | tf_op jit(solution)/shard_map/ppermute | solution.py:25
  75.0 1.8 %collective-permute-done.25 = f32[1,4,32]{2,1,0:T(4,128)S(1)} collective-permute-done((f32[1,4,32]{2,1,0:T(4,128)S(1)}, f32[1,4,32]{2,1,0:T(4,128)S(1)}, u32[]{:S(2)}, u32[]{:S(2)}) %collective-permute-start.25) | collective-permute-done | bytes 544 | tf_op jit(solution)/shard_map/ppermute | solution.py:23
  78.2 3.6 %collective-permute-done.27 = f32[8,1,32]{2,1,0:T(1,128)S(1)} collective-permute-done((f32[8,1,32]{2,1,0:T(1,128)S(1)}, f32[8,1,32]{2,1,0:T(1,128)S(1)}, u32[]{:S(2)}, u32[]{:S(2)}) %collective-permute-start.27) | collective-permute-done | bytes 1056 | tf_op jit(solution)/shard_map/ppermute | solution.py:23
  82.5 1.2 %collective-permute-start.28 = (f32[1,16,128]{2,1,0:T(8,128)S(1)}, f32[1,16,128]{2,1,0:T(8,128)S(1)}, u32[]{:S(2)}, u32[]{:S(2)}) collective-permute-start(f32[1,16,128]{2,1,0:T(8,128)S(1)} %get-tuple-element.160), channel_id=1, source_target_pairs={{8,0},{16,8},{24,16},{0,24},{9,1},{17,9},{25,17},{1,25},{10,2},{18... | collective-permute-start | bytes 24584 | tf_op jit(solution)/shard_map/ppermute | solution.py:25
  84.6 1.6 %collective-permute-done.28 = f32[1,16,128]{2,1,0:T(8,128)S(1)} collective-permute-done((f32[1,16,128]{2,1,0:T(8,128)S(1)}, f32[1,16,128]{2,1,0:T(8,128)S(1)}, u32[]{:S(2)}, u32[]{:S(2)}) %collective-permute-start.28) | collective-permute-done | bytes 8224 | tf_op jit(solution)/shard_map/ppermute | solution.py:25
  86.2 2.0 %collective-permute-done.29 = f32[1,16,128]{2,1,0:T(8,128)S(1)} collective-permute-done((f32[1,16,128]{2,1,0:T(8,128)S(1)}, f32[1,16,128]{2,1,0:T(8,128)S(1)}, u32[]{:S(2)}, u32[]{:S(2)}) %collective-permute-start.29) | collective-permute-done | bytes 8224 | tf_op jit(solution)/shard_map/ppermute | solution.py:23
  89.7 3.6 %collective-permute-done.31 = f32[26,1,128]{2,1,0:T(1,128)S(1)} collective-permute-done((f32[26,1,128]{2,1,0:T(1,128)S(1)}, f32[26,1,128]{2,1,0:T(1,128)S(1)}, u32[]{:S(2)}, u32[]{:S(2)}) %collective-permute-start.31) | collective-permute-done | bytes 13344 | tf_op jit(solution)/shard_map/ppermute | solution.py:23
  96.6 1.6 %collective-permute-done.32 = f32[1,16,128]{2,1,0:T(8,128)S(1)} collective-permute-done((f32[1,16,128]{2,1,0:T(8,128)S(1)}, f32[1,16,128]{2,1,0:T(8,128)S(1)}, u32[]{:S(2)}, u32[]{:S(2)}) %collective-permute-start.32) | collective-permute-done | bytes 8224 | tf_op jit(solution)/shard_map/ppermute | solution.py:25
  98.2 1.8 %collective-permute-done.33 = f32[1,16,128]{2,1,0:T(8,128)S(1)} collective-permute-done((f32[1,16,128]{2,1,0:T(8,128)S(1)}, f32[1,16,128]{2,1,0:T(8,128)S(1)}, u32[]{:S(2)}, u32[]{:S(2)}) %collective-permute-start.33) | collective-permute-done | bytes 8224 | tf_op jit(solution)/shard_map/ppermute | solution.py:23
  101.5 3.6 %collective-permute-done.35 = f32[26,1,128]{2,1,0:T(1,128)S(1)} collective-permute-done((f32[26,1,128]{2,1,0:T(1,128)S(1)}, f32[26,1,128]{2,1,0:T(1,128)S(1)}, u32[]{:S(2)}, u32[]{:S(2)}) %collective-permute-start.35) | collective-permute-done | bytes 13344 | tf_op jit(solution)/shard_map/ppermute | solution.py:23
  106.6 1.8 %collective-permute-start.37 = (f32[1,16,128]{2,1,0:T(8,128)S(1)}, f32[1,16,128]{2,1,0:T(8,128)S(1)}, u32[]{:S(2)}, u32[]{:S(2)}) collective-permute-start(f32[1,16,128]{2,1,0:T(8,128)S(1)} %get-tuple-element.141), channel_id=1, source_target_pairs={{0,8},{8,16},{16,24},{24,0},{1,9},{9,17},{17,25},{25,1},{2,10},{10... | collective-permute-start | bytes 24584 | tf_op jit(solution)/shard_map/ppermute | solution.py:23
  108.4 1.6 %collective-permute-done.36 = f32[1,16,128]{2,1,0:T(8,128)S(1)} collective-permute-done((f32[1,16,128]{2,1,0:T(8,128)S(1)}, f32[1,16,128]{2,1,0:T(8,128)S(1)}, u32[]{:S(2)}, u32[]{:S(2)}) %collective-permute-start.36) | collective-permute-done | bytes 8224 | tf_op jit(solution)/shard_map/ppermute | solution.py:25
  110.0 1.1 collective-permute-done.37
  112.6 3.6 %collective-permute-done.39 = f32[26,1,128]{2,1,0:T(1,128)S(1)} collective-permute-done((f32[26,1,128]{2,1,0:T(1,128)S(1)}, f32[26,1,128]{2,1,0:T(1,128)S(1)}, u32[]{:S(2)}, u32[]{:S(2)}) %collective-permute-start.39) | collective-permute-done | bytes 13344 | tf_op jit(solution)/shard_map/ppermute | solution.py:23
  116.8 1.3 %fusion.9 = f32[24,16,128]{2,1,0:T(8,128)} fusion(f32[24,16,128]{2,1,0:T(8,128)S(1)} %get-tuple-element.6, f32[24,16,128]{2,1,0:T(8,128)S(1)} %get-tuple-element.7, f32[1,16,128]{2,1,0:T(8,128)S(1)} %collective-permute-done.37, f32[1,16,128]{2,1,0:T(8,128)S(1)} %collective-permute-done.36, f32[24,16,128]{2,1,0:T(8,128)S(1)} %get-tuple-element.9, ...), kind=kLoop, calls=%fused_computation.114 | loop fusion | flops 2359296 | bytes 4541440 | tf_op jit(solution)/shard_map/sub | solution.py:162
  (187 shorter events, 43.5 us)
Async XLA Ops:
  1.3 9.9 %collective-permute-start.1 = (f32[1,16,128]{2,1,0:T(8,128)S(1)}, f32[1,16,128]{2,1,0:T(8,128)S(1)}, u32[]{:S(2)}, u32[]{:S(2)}) collective-permute-start(f32[1,16,128]{2,1,0:T(8,128)S(1)} %get-tuple-element.192), channel_id=1, source_target_pairs={{0,8},{8,16},{16,24},{24,0},{1,9},{9,17},{17,25},{25,1},{2,10},{10... | collective-permute-start | bytes 24584 | tf_op jit(solution)/shard_map/ppermute | solution.py:23
  4.3 7.0 %collective-permute-start = (f32[1,16,128]{2,1,0:T(8,128)S(1)}, f32[1,16,128]{2,1,0:T(8,128)S(1)}, u32[]{:S(2)}, u32[]{:S(2)}) collective-permute-start(f32[1,16,128]{2,1,0:T(8,128)S(1)} %get-tuple-element.191), channel_id=1, source_target_pairs={{8,0},{16,8},{24,16},{0,24},{9,1},{17,9},{25,17},{1,25},{10,2},{18... | collective-permute-start | bytes 24584 | tf_op jit(solution)/shard_map/ppermute | solution.py:25
  6.0 5.6 %collective-permute-start.5 = (f32[1,16,128]{2,1,0:T(8,128)S(1)}, f32[1,16,128]{2,1,0:T(8,128)S(1)}, u32[]{:S(2)}, u32[]{:S(2)}) collective-permute-start(f32[1,16,128]{2,1,0:T(8,128)S(1)} %get-tuple-element.201), channel_id=1, source_target_pairs={{0,8},{8,16},{16,24},{24,0},{1,9},{9,17},{17,25},{25,1},{2,10},{10... | collective-permute-start | bytes 24584 | tf_op jit(solution)/shard_map/ppermute | solution.py:23
  7.0 4.6 %collective-permute-start.4 = (f32[1,16,128]{2,1,0:T(8,128)S(1)}, f32[1,16,128]{2,1,0:T(8,128)S(1)}, u32[]{:S(2)}, u32[]{:S(2)}) collective-permute-start(f32[1,16,128]{2,1,0:T(8,128)S(1)} %get-tuple-element.200), channel_id=1, source_target_pairs={{8,0},{16,8},{24,16},{0,24},{9,1},{17,9},{25,17},{1,25},{10,2},{18... | collective-permute-start | bytes 24584 | tf_op jit(solution)/shard_map/ppermute | solution.py:25
  12.4 6.1 %collective-permute-start.2 = (f32[26,1,128]{2,1,0:T(1,128)S(1)}, f32[26,1,128]{2,1,0:T(1,128)S(1)}, u32[]{:S(2)}, u32[]{:S(2)}) collective-permute-start(f32[26,1,128]{2,1,0:T(1,128)S(1)} %get-tuple-element.88), channel_id=1, source_target_pairs={{1,0},{2,1},{3,2},{4,3},{5,4},{6,5},{7,6},{0,7},{9,8},{10,9},{11,1... | collective-permute-start | bytes 39944 | tf_op jit(solution)/shard_map/ppermute | solution.py:25
  14.8 4.9 %collective-permute-start.3 = (f32[26,1,128]{2,1,0:T(1,128)S(1)}, f32[26,1,128]{2,1,0:T(1,128)S(1)}, u32[]{:S(2)}, u32[]{:S(2)}) collective-permute-start(f32[26,1,128]{2,1,0:T(1,128)S(1)} %get-tuple-element.89), channel_id=1, source_target_pairs={{0,1},{1,2},{2,3},{3,4},{4,5},{5,6},{6,7},{7,0},{8,9},{9,10},{10,1... | collective-permute-start | bytes 39944 | tf_op jit(solution)/shard_map/ppermute | solution.py:23
  14.9 5.3 %collective-permute-start.6 = (f32[26,1,128]{2,1,0:T(1,128)S(1)}, f32[26,1,128]{2,1,0:T(1,128)S(1)}, u32[]{:S(2)}, u32[]{:S(2)}) collective-permute-start(f32[26,1,128]{2,1,0:T(1,128)S(1)} %get-tuple-element.94), channel_id=1, source_target_pairs={{1,0},{2,1},{3,2},{4,3},{5,4},{6,5},{7,6},{0,7},{9,8},{10,9},{11,1... | collective-permute-start | bytes 39944 | tf_op jit(solution)/shard_map/ppermute | solution.py:25
  18.5 4.9 %collective-permute-start.7 = (f32[26,1,128]{2,1,0:T(1,128)S(1)}, f32[26,1,128]{2,1,0:T(1,128)S(1)}, u32[]{:S(2)}, u32[]{:S(2)}) collective-permute-start(f32[26,1,128]{2,1,0:T(1,128)S(1)} %get-tuple-element.95), channel_id=1, source_target_pairs={{0,1},{1,2},{2,3},{3,4},{4,5},{5,6},{6,7},{7,0},{8,9},{9,10},{10,1... | collective-permute-start | bytes 39944 | tf_op jit(solution)/shard_map/ppermute | solution.py:23
  26.1 3.7 %collective-permute-start.8 = (f32[1,16,128]{2,1,0:T(8,128)S(1)}, f32[1,16,128]{2,1,0:T(8,128)S(1)}, u32[]{:S(2)}, u32[]{:S(2)}) collective-permute-start(f32[1,16,128]{2,1,0:T(8,128)S(1)} %get-tuple-element.180), channel_id=1, source_target_pairs={{8,0},{16,8},{24,16},{0,24},{9,1},{17,9},{25,17},{1,25},{10,2},{18... | collective-permute-start | bytes 24584 | tf_op jit(solution)/shard_map/ppermute | solution.py:25
  27.1 4.5 %collective-permute-start.9 = (f32[1,16,128]{2,1,0:T(8,128)S(1)}, f32[1,16,128]{2,1,0:T(8,128)S(1)}, u32[]{:S(2)}, u32[]{:S(2)}) collective-permute-start(f32[1,16,128]{2,1,0:T(8,128)S(1)} %get-tuple-element.181), channel_id=1, source_target_pairs={{0,8},{8,16},{16,24},{24,0},{1,9},{9,17},{17,25},{25,1},{2,10},{10... | collective-permute-start | bytes 24584 | tf_op jit(solution)/shard_map/ppermute | solution.py:23
  31.7 5.0 %collective-permute-start.11 = (f32[26,1,128]{2,1,0:T(1,128)S(1)}, f32[26,1,128]{2,1,0:T(1,128)S(1)}, u32[]{:S(2)}, u32[]{:S(2)}) collective-permute-start(f32[26,1,128]{2,1,0:T(1,128)S(1)} %get-tuple-element.83), channel_id=1, source_target_pairs={{0,1},{1,2},{2,3},{3,4},{4,5},{5,6},{6,7},{7,0},{8,9},{9,10},{10,1... | collective-permute-start | bytes 39944 | tf_op jit(solution)/shard_map/ppermute | solution.py:23
  37.8 3.7 %collective-permute-start.12 = (f32[1,16,128]{2,1,0:T(8,128)S(1)}, f32[1,16,128]{2,1,0:T(8,128)S(1)}, u32[]{:S(2)}, u32[]{:S(2)}) collective-permute-start(f32[1,16,128]{2,1,0:T(8,128)S(1)} %get-tuple-element.170), channel_id=1, source_target_pairs={{8,0},{16,8},{24,16},{0,24},{9,1},{17,9},{25,17},{1,25},{10,2},{18... | collective-permute-start | bytes 24584 | tf_op jit(solution)/shard_map/ppermute | solution.py:25
  39.0 4.5 %collective-permute-start.13 = (f32[1,16,128]{2,1,0:T(8,128)S(1)}, f32[1,16,128]{2,1,0:T(8,128)S(1)}, u32[]{:S(2)}, u32[]{:S(2)}) collective-permute-start(f32[1,16,128]{2,1,0:T(8,128)S(1)} %get-tuple-element.171), channel_id=1, source_target_pairs={{0,8},{8,16},{16,24},{24,0},{1,9},{9,17},{17,25},{25,1},{2,10},{10... | collective-permute-start | bytes 24584 | tf_op jit(solution)/shard_map/ppermute | solution.py:23
  43.6 5.0 %collective-permute-start.15 = (f32[26,1,128]{2,1,0:T(1,128)S(1)}, f32[26,1,128]{2,1,0:T(1,128)S(1)}, u32[]{:S(2)}, u32[]{:S(2)}) collective-permute-start(f32[26,1,128]{2,1,0:T(1,128)S(1)} %get-tuple-element.79), channel_id=1, source_target_pairs={{0,1},{1,2},{2,3},{3,4},{4,5},{5,6},{6,7},{7,0},{8,9},{9,10},{10,1... | collective-permute-start | bytes 39944 | tf_op jit(solution)/shard_map/ppermute | solution.py:23
  50.3 3.6 %collective-permute-start.16 = (f32[1,4,32]{2,1,0:T(4,128)S(1)}, f32[1,4,32]{2,1,0:T(4,128)S(1)}, u32[]{:S(2)}, u32[]{:S(2)}) collective-permute-start(f32[1,4,32]{2,1,0:T(4,128)S(1)} %get-tuple-element.283), channel_id=1, source_target_pairs={{8,0},{16,8},{24,16},{0,24},{9,1},{17,9},{25,17},{1,25},{10,2},{18... | collective-permute-start | bytes 1544 | tf_op jit(solution)/shard_map/ppermute | solution.py:25
  51.3 4.5 %collective-permute-start.17 = (f32[1,4,32]{2,1,0:T(4,128)S(1)}, f32[1,4,32]{2,1,0:T(4,128)S(1)}, u32[]{:S(2)}, u32[]{:S(2)}) collective-permute-start(f32[1,4,32]{2,1,0:T(4,128)S(1)} %get-tuple-element.282), channel_id=1, source_target_pairs={{0,8},{8,16},{16,24},{24,0},{1,9},{9,17},{17,25},{25,1},{2,10},{10... | collective-permute-start | bytes 1544 | tf_op jit(solution)/shard_map/ppermute | solution.py:23
  55.8 4.9 %collective-permute-start.19 = (f32[8,1,32]{2,1,0:T(1,128)S(1)}, f32[8,1,32]{2,1,0:T(1,128)S(1)}, u32[]{:S(2)}, u32[]{:S(2)}) collective-permute-start(f32[8,1,32]{2,1,0:T(1,128)S(1)} %get-tuple-element.237), channel_id=1, source_target_pairs={{0,1},{1,2},{2,3},{3,4},{4,5},{5,6},{6,7},{7,0},{8,9},{9,10},{10,1... | collective-permute-start | bytes 3080 | tf_op jit(solution)/shard_map/ppermute | solution.py:23
  61.2 3.6 %collective-permute-start.20 = (f32[1,4,32]{2,1,0:T(4,128)S(1)}, f32[1,4,32]{2,1,0:T(4,128)S(1)}, u32[]{:S(2)}, u32[]{:S(2)}) collective-permute-start(f32[1,4,32]{2,1,0:T(4,128)S(1)} %get-tuple-element.271), channel_id=1, source_target_pairs={{8,0},{16,8},{24,16},{0,24},{9,1},{17,9},{25,17},{1,25},{10,2},{18... | collective-permute-start | bytes 1544 | tf_op jit(solution)/shard_map/ppermute | solution.py:25
  61.4 4.5 %collective-permute-start.21 = (f32[1,4,32]{2,1,0:T(4,128)S(1)}, f32[1,4,32]{2,1,0:T(4,128)S(1)}, u32[]{:S(2)}, u32[]{:S(2)}) collective-permute-start(f32[1,4,32]{2,1,0:T(4,128)S(1)} %get-tuple-element.270), channel_id=1, source_target_pairs={{0,8},{8,16},{16,24},{24,0},{1,9},{9,17},{17,25},{25,1},{2,10},{10... | collective-permute-start | bytes 1544 | tf_op jit(solution)/shard_map/ppermute | solution.py:23
  66.0 4.9 %collective-permute-start.23 = (f32[8,1,32]{2,1,0:T(1,128)S(1)}, f32[8,1,32]{2,1,0:T(1,128)S(1)}, u32[]{:S(2)}, u32[]{:S(2)}) collective-permute-start(f32[8,1,32]{2,1,0:T(1,128)S(1)} %get-tuple-element.233), channel_id=1, source_target_pairs={{0,1},{1,2},{2,3},{3,4},{4,5},{5,6},{6,7},{7,0},{8,9},{9,10},{10,1... | collective-permute-start | bytes 3080 | tf_op jit(solution)/shard_map/ppermute | solution.py:23
  71.3 3.6 %collective-permute-start.24 = (f32[1,4,32]{2,1,0:T(4,128)S(1)}, f32[1,4,32]{2,1,0:T(4,128)S(1)}, u32[]{:S(2)}, u32[]{:S(2)}) collective-permute-start(f32[1,4,32]{2,1,0:T(4,128)S(1)} %get-tuple-element.258), channel_id=1, source_target_pairs={{8,0},{16,8},{24,16},{0,24},{9,1},{17,9},{25,17},{1,25},{10,2},{18... | collective-permute-start | bytes 1544 | tf_op jit(solution)/shard_map/ppermute | solution.py:25
  72.3 4.5 %collective-permute-start.25 = (f32[1,4,32]{2,1,0:T(4,128)S(1)}, f32[1,4,32]{2,1,0:T(4,128)S(1)}, u32[]{:S(2)}, u32[]{:S(2)}) collective-permute-start(f32[1,4,32]{2,1,0:T(4,128)S(1)} %get-tuple-element.259), channel_id=1, source_target_pairs={{0,8},{8,16},{16,24},{24,0},{1,9},{9,17},{17,25},{25,1},{2,10},{10... | collective-permute-start | bytes 1544 | tf_op jit(solution)/shard_map/ppermute | solution.py:23
  76.9 4.9 %collective-permute-start.27 = (f32[8,1,32]{2,1,0:T(1,128)S(1)}, f32[8,1,32]{2,1,0:T(1,128)S(1)}, u32[]{:S(2)}, u32[]{:S(2)}) collective-permute-start(f32[8,1,32]{2,1,0:T(1,128)S(1)} %get-tuple-element.229), channel_id=1, source_target_pairs={{0,1},{1,2},{2,3},{3,4},{4,5},{5,6},{6,7},{7,0},{8,9},{9,10},{10,1... | collective-permute-start | bytes 3080 | tf_op jit(solution)/shard_map/ppermute | solution.py:23
  82.5 3.7 %collective-permute-start.28 = (f32[1,16,128]{2,1,0:T(8,128)S(1)}, f32[1,16,128]{2,1,0:T(8,128)S(1)}, u32[]{:S(2)}, u32[]{:S(2)}) collective-permute-start(f32[1,16,128]{2,1,0:T(8,128)S(1)} %get-tuple-element.160), channel_id=1, source_target_pairs={{8,0},{16,8},{24,16},{0,24},{9,1},{17,9},{25,17},{1,25},{10,2},{18... | collective-permute-start | bytes 24584 | tf_op jit(solution)/shard_map/ppermute | solution.py:25
  83.7 4.6 %collective-permute-start.29 = (f32[1,16,128]{2,1,0:T(8,128)S(1)}, f32[1,16,128]{2,1,0:T(8,128)S(1)}, u32[]{:S(2)}, u32[]{:S(2)}) collective-permute-start(f32[1,16,128]{2,1,0:T(8,128)S(1)} %get-tuple-element.161), channel_id=1, source_target_pairs={{0,8},{8,16},{16,24},{24,0},{1,9},{9,17},{17,25},{25,1},{2,10},{10... | collective-permute-start | bytes 24584 | tf_op jit(solution)/shard_map/ppermute | solution.py:23
  88.3 5.0 %collective-permute-start.31 = (f32[26,1,128]{2,1,0:T(1,128)S(1)}, f32[26,1,128]{2,1,0:T(1,128)S(1)}, u32[]{:S(2)}, u32[]{:S(2)}) collective-permute-start(f32[26,1,128]{2,1,0:T(1,128)S(1)} %get-tuple-element.75), channel_id=1, source_target_pairs={{0,1},{1,2},{2,3},{3,4},{4,5},{5,6},{6,7},{7,0},{8,9},{9,10},{10,1... | collective-permute-start | bytes 39944 | tf_op jit(solution)/shard_map/ppermute | solution.py:23
  94.5 3.7 %collective-permute-start.32 = (f32[1,16,128]{2,1,0:T(8,128)S(1)}, f32[1,16,128]{2,1,0:T(8,128)S(1)}, u32[]{:S(2)}, u32[]{:S(2)}) collective-permute-start(f32[1,16,128]{2,1,0:T(8,128)S(1)} %get-tuple-element.150), channel_id=1, source_target_pairs={{8,0},{16,8},{24,16},{0,24},{9,1},{17,9},{25,17},{1,25},{10,2},{18... | collective-permute-start | bytes 24584 | tf_op jit(solution)/shard_map/ppermute | solution.py:25
  95.5 4.5 %collective-permute-start.33 = (f32[1,16,128]{2,1,0:T(8,128)S(1)}, f32[1,16,128]{2,1,0:T(8,128)S(1)}, u32[]{:S(2)}, u32[]{:S(2)}) collective-permute-start(f32[1,16,128]{2,1,0:T(8,128)S(1)} %get-tuple-element.151), channel_id=1, source_target_pairs={{0,8},{8,16},{16,24},{24,0},{1,9},{9,17},{17,25},{25,1},{2,10},{10... | collective-permute-start | bytes 24584 | tf_op jit(solution)/shard_map/ppermute | solution.py:23
  100.1 5.0 %collective-permute-start.35 = (f32[26,1,128]{2,1,0:T(1,128)S(1)}, f32[26,1,128]{2,1,0:T(1,128)S(1)}, u32[]{:S(2)}, u32[]{:S(2)}) collective-permute-start(f32[26,1,128]{2,1,0:T(1,128)S(1)} %get-tuple-element.71), channel_id=1, source_target_pairs={{0,1},{1,2},{2,3},{3,4},{4,5},{5,6},{6,7},{7,0},{8,9},{9,10},{10,1... | collective-permute-start | bytes 39944 | tf_op jit(solution)/shard_map/ppermute | solution.py:23
  106.3 3.7 %collective-permute-start.36 = (f32[1,16,128]{2,1,0:T(8,128)S(1)}, f32[1,16,128]{2,1,0:T(8,128)S(1)}, u32[]{:S(2)}, u32[]{:S(2)}) collective-permute-start(f32[1,16,128]{2,1,0:T(8,128)S(1)} %get-tuple-element.140), channel_id=1, source_target_pairs={{8,0},{16,8},{24,16},{0,24},{9,1},{17,9},{25,17},{1,25},{10,2},{18... | collective-permute-start | bytes 24584 | tf_op jit(solution)/shard_map/ppermute | solution.py:25
  106.6 4.5 %collective-permute-start.37 = (f32[1,16,128]{2,1,0:T(8,128)S(1)}, f32[1,16,128]{2,1,0:T(8,128)S(1)}, u32[]{:S(2)}, u32[]{:S(2)}) collective-permute-start(f32[1,16,128]{2,1,0:T(8,128)S(1)} %get-tuple-element.141), channel_id=1, source_target_pairs={{0,8},{8,16},{16,24},{24,0},{1,9},{9,17},{17,25},{25,1},{2,10},{10... | collective-permute-start | bytes 24584 | tf_op jit(solution)/shard_map/ppermute | solution.py:23
  111.2 5.0 %collective-permute-start.39 = (f32[26,1,128]{2,1,0:T(1,128)S(1)}, f32[26,1,128]{2,1,0:T(1,128)S(1)}, u32[]{:S(2)}, u32[]{:S(2)}) collective-permute-start(f32[26,1,128]{2,1,0:T(1,128)S(1)} %get-tuple-element.67), channel_id=1, source_target_pairs={{0,1},{1,2},{2,3},{3,4},{4,5},{5,6},{6,7},{7,0},{8,9},{9,10},{10,1... | collective-permute-start | bytes 39944 | tf_op jit(solution)/shard_map/ppermute | solution.py:23
  (12 other events, 26.9 us)
where the time goes:
time: 118 us
  waiting for transfers between devices  61.1 us (52%)
  starting transfers between devices  33.9 us (29%)
  other arithmetic  10.3 us (9%)
  local copies, waits for them, and re-layouts  9.42 us (8%)
  matrix products  1.92 us (2%)
  between operations  1.42 us (1%)
    ppermute x20, waiting for transfers between devices, extended_2(): lax.ppermute(tail, axis, [(i, (i + 1) % count) for i in range(count)])  46.6 us
    ppermute x20, starting transfers between devices, extended_2(): lax.ppermute(tail, axis, [(i, (i + 1) % count) for i in range(count)])  17.8 us
    ppermute x20, starting transfers between devices, extended_2(): lax.ppermute(head, axis, [((i + 1) % count, i) for i in range(count)])  16.1 us
    ppermute x20, waiting for transfers between devices, extended_2(): lax.ppermute(head, axis, [((i + 1) % count, i) for i in range(count)])  14.4 us
    slice x42, local copies, waits for them, and re-layouts, getter(): return jnp.roll(window, -shift_z, axis=2)  5.49 us
    concatenate x24, other arithmetic, extended_2(): jnp.concatenate([lax.ppermute(tail, axis, [(i, (i + 1) % count) for i in...  3.56 us
    add x6, other arithmetic, relax_padded(): centre + damping * (source - operate(cropper(padded), coeffs, spacing)) /...  3.5 us
  transfers between devices with their start and end apart: 40, of which 34 were waited for; matrix products, arithmetic and copies ran while one was open for 7% of the time, Pallas kernels for 0%

commit v1 on v0

v1 whole, which is shorter than its diff:
```python
import functools

import jax
import jax.numpy as jnp
from jax import lax
from jax.experimental import pallas as pl
from jax.experimental.pallas import tpu as pltpu
from jax.sharding import PartitionSpec as P

MESH = pl.DeviceIdType.MESH
SCREEN = 0.002
DAMP = 0.6
F32 = jnp.float32
NEIGHBOURS = [(-1, -1), (-1, 0), (-1, 1), (0, -1), (0, 1), (1, -1), (1, 0), (1, 1)]


def first_plane(ref, at):
    v = ref[at]
    rows = v.shape[0]
    zp = pltpu.roll(v, v.shape[1] - 1, 1)
    zm = pltpu.roll(v, 1, 1)
    yp = pltpu.roll(v, rows - 1, 0)
    ym = pltpu.roll(v, 1, 0)
    dz = zp - zm
    dyz = pltpu.roll(dz, rows - 1, 0) - pltpu.roll(dz, 1, 0)
    return v, dz, yp - ym, zp + zm, yp + ym, dyz


def walk(ref, low, high, emit, unroll=2):
    def step(at, carry):
        before, here = carry
        after = first_plane(ref, at + 1)
        emit(
            at,
            here[0],
            before[0] + after[0],
            here[4],
            here[3],
            after[2] - before[2],
            after[1] - before[1],
            here[5],
        )
        return here[:3], after

    start = (first_plane(ref, low - 1)[:3], first_plane(ref, low))
    lax.fori_loop(low, high, step, start, unroll=unroll)


def dot_exact(values, table):
    hi = values.astype(jnp.bfloat16)
    rest = values - hi.astype(F32)
    mid = rest.astype(jnp.bfloat16)
    lo = (rest - mid.astype(F32)).astype(jnp.bfloat16)
    n = values.shape[0]
    out = jnp.dot(jnp.concatenate([hi, mid, lo], axis=0), table, preferred_element_type=F32)
    return out[:n] + out[n : 2 * n] + out[2 * n :]


def kernel(
    gx_n, gy_n, p_in, d_in, c_in, up_out, res_out,
    pot, cor, den, coef, wgt, src, one, two, fin,
    msg_lo, msg_hi, got_lo, got_hi, est_lo, est_hi,
    pool_c, pool_s, co, cs, got_co, got_cs, wide, grown,
    in_sem, s1, r1, s2, r2, sc, rc, ss, rs,
):
    nx, ny, nz = p_in.shape
    x0, x1 = 4, 4 + nx
    gx = lax.axis_index("gx")
    gy = lax.axis_index("gy")

    def device(dx, dy):
        return (lax.rem(gx + dx + gx_n, gx_n), lax.rem(gy + dy + gy_n, gy_n))

    loads = []
    for k, (a, b) in enumerate(((p_in, pot), (c_in, cor), (d_in, den))):
        copy = pltpu.make_async_copy(a, b.at[x0:x1, 0:ny], in_sem.at[k])
        copy.start()
        loads.append(copy)
    barrier = pltpu.get_barrier_semaphore()
    for dx, dy in NEIGHBOURS:
        pl.semaphore_signal(barrier, inc=1, device_id=device(dx, dy), device_id_type=MESH)

    sub = lax.broadcasted_iota(jnp.int32, (8, nz), 0)
    wide[:, :, 14:16, :] = jnp.zeros((7, 3, 2, nz), F32)
    for f in range(6):
        pool_c[(f * 8 + 6) * ny : (f * 8 + 8) * ny, :] = jnp.zeros((2 * ny, nz), F32)
    pool_s[6 * ny : 8 * ny, :] = jnp.zeros((2 * ny, nz), F32)

    for copy in loads:
        copy.wait()

    def pack(x, _):
        top = ny - 8
        p, c, d = pot[x0 + x, top:ny], cor[x0 + x, top:ny], den[x0 + x, top:ny]
        msg_lo[x] = jnp.where(
            sub >= 5, p, jnp.where(sub >= 2, pltpu.roll(c, 5, 0), pltpu.roll(d, 2, 0))
        )
        p, c, d = pot[x0 + x, 0:8], cor[x0 + x, 0:8], den[x0 + x, 0:8]
        msg_hi[x] = jnp.where(
            sub < 3, p, jnp.where(sub < 6, pltpu.roll(c, 3, 0), pltpu.roll(d, 6, 0))
        )
        return 0

    lax.fori_loop(0, nx, pack, 0, unroll=4)
    pl.semaphore_wait(barrier, 8)

    def remote(a, b, send, recv, k, to):
        copy = pltpu.make_async_remote_copy(
            src_ref=a, dst_ref=b, send_sem=send.at[k], recv_sem=recv.at[k],
            device_id=to, device_id_type=MESH,
        )
        copy.start()
        return copy

    def y_sends(low, high, into_low, into_high, send, recv, k):
        out = []
        for dy, part, into in ((1, low, into_low), (-1, high, into_high)):
            out.append(remote(part(0, nx), into.at[x0:x1], send, recv, k, device(0, dy)))
            out.append(remote(part(0, 3), into.at[x1 : x1 + 3], send, recv, k + 1, device(-1, dy)))
            out.append(remote(part(nx - 3, nx), into.at[1:x0], send, recv, k + 2, device(1, dy)))
            k += 3
        return out

    round_1 = []
    k = 0
    for ref, width in ((pot, 3), (cor, 3), (den, 2)):
        round_1.append(remote(
            ref.at[x1 - width : x1, 0:ny], ref.at[x0 - width : x0, 0:ny], s1, r1, k, device(1, 0)))
        round_1.append(remote(
            ref.at[x0 : x0 + width, 0:ny], ref.at[x1 : x1 + width, 0:ny], s1, r1, k + 1, device(-1, 0)))
        k += 2
    round_1 += y_sends(
        lambda a, b: msg_lo.at[a:b], lambda a, b: msg_hi.at[a:b], got_lo, got_hi, s1, r1, k)

    rows_at = lax.broadcasted_iota(jnp.int32, (4 * nz, nz), 0)
    cols_at = lax.broadcasted_iota(jnp.int32, (4 * nz, nz), 1)
    group = nz // 4
    mean_table = jnp.where(
        (rows_at // nz) * group + (rows_at % nz) // 4 == cols_at, 1.0 / 64.0, 0.0
    ).astype(jnp.bfloat16)

    def pooled(ref, count):
        parts = []
        for y in range(4):
            total = ref[pl.ds(4 * y, count, stride=ny), :]
            for j in range(1, 4):
                total = total + ref[pl.ds(4 * y + j, count, stride=ny), :]
            parts.append(total)
        return dot_exact(jnp.concatenate(parts, axis=1), mean_table)

    for copy in round_1:
        copy.wait_recv()

    def unpack(at, _):
        lo, hi = got_lo[at], got_hi[at]
        pot[at, ny : ny + 8] = jnp.where(sub < 4, hi, lo)
        cor[at, ny : ny + 8] = jnp.where(sub < 4, pltpu.roll(hi, 5, 0), pltpu.roll(lo, 3, 0))
        den[at, ny : ny + 8] = jnp.where(sub < 4, pltpu.roll(hi, 2, 0), pltpu.roll(lo, 6, 0))
        return 0

    lax.fori_loop(1, x1 + 3, unpack, 0, unroll=3)

    def build(at, v, xs, ys, zs, dxy, dxz, dyz):
        twice = 2.0 * v
        xx, yy, zz = 1.0 + (xs - twice), 1.0 + (ys - twice), 1.0 + (zs - twice)
        xy, xz, yz = 0.25 * dxy, 0.25 * dxz, 0.25 * dyz
        cxx = yy * zz - yz * yz
        cyy = xx * zz - xz * xz
        czz = xx * yy - xy * xy
        cxy = xz * yz - xy * zz
        cxz = xy * yz - xz * yy
        cyz = xy * xz - xx * yz
        src[at] = den[at] - (xx * cxx + xy * cxy + xz * cxz)
        wgt[at] = DAMP / (-2.0 * (cxx + cyy + czz) - SCREEN)
        coef[0, at], coef[1, at], coef[2, at] = cxx, cyy, czz
        coef[3, at], coef[4, at], coef[5, at] = 0.5 * cxy, 0.5 * cxz, 0.5 * cyz

    walk(pot, x0 - 2, x1 + 2, build)

    def pool_coef(i, _):
        for f in range(6):
            total = coef[f, x0 + 4 * i, 0:ny]
            for j in range(1, 4):
                total = total + coef[f, x0 + 4 * i + j, 0:ny]
            pool_c[pl.ds(pl.multiple_of((f * 8 + i) * ny, 8), ny), :] = total
        return 0

    lax.fori_loop(0, nx // 4, pool_coef, 0)
    co[...] = pooled(pool_c, 48).reshape(6, 8, nz)
    coarse_c = [
        remote(co, got_co.at[7 - k], sc, rc, k, device(*NEIGHBOURS[k])) for k in range(8)
    ]

    def off_diagonal(at, xs, ys, zs, dxy, dxz, dyz):
        return (
            (coef[0, at] * xs + coef[1, at] * ys + coef[2, at] * zs)
            + (coef[3, at] * dxy + coef[4, at] * dxz + coef[5, at] * dyz)
        )

    def sweep(a, b, low, high):
        def emit(at, v, *terms):
            b[at] = (1.0 - DAMP) * v + wgt[at] * (src[at] - off_diagonal(at, *terms))

        walk(a, low, high, emit)

    def residual_at(at, v, *terms):
        n = ny
        cut = [t[0:n] for t in terms]
        c = [coef[f, at, 0:n] for f in range(6)]
        main = -2.0 * (c[0] + c[1] + c[2]) - SCREEN
        total = c[0] * cut[0] + c[1] * cut[1] + c[2] * cut[2]
        total = total + (c[3] * cut[3] + c[4] * cut[4] + c[5] * cut[5])
        return src[at, 0:n] - (total + main * v[0:n])

    sweep(cor, one, x0 - 2, x1 + 2)
    sweep(one, two, x0 - 1, x1 + 1)

    round_2 = [
        remote(two.at[x1 - 3 : x1, 0:ny], fin.at[1:x0, 0:ny], s2, r2, 0, device(1, 0)),
        remote(two.at[x0 : x0 + 3, 0:ny], fin.at[x1 : x1 + 3, 0:ny], s2, r2, 1, device(-1, 0)),
    ] + y_sends(
        lambda a, b: two.at[x0 + a : x0 + b, ny - 8 : ny],
        lambda a, b: two.at[x0 + a : x0 + b, 0:8],
        est_lo, est_hi, s2, r2, 2)

    def emit_first(at, v, *terms):
        res_out[at - x0] = residual_at(at, v, *terms)

    walk(two, x0, x1, emit_first)
    for i in range(nx // 4):
        pool_s[i * ny : (i + 1) * ny, :] = (
            (res_out[4 * i] + res_out[4 * i + 1]) + (res_out[4 * i + 2] + res_out[4 * i + 3])
        )
    cs[...] = pooled(pool_s, 8)
    coarse_s = [
        remote(cs, got_cs.at[7 - k], ss, rs, k, device(*NEIGHBOURS[k])) for k in range(8)
    ]

    def place(field, at_y, dx, value):
        if dx < 0:
            wide[field, at_y, 0:4, :] = value[2:6]
        elif dx == 0:
            wide[field, at_y, 4:10, :] = value[0:6]
        else:
            wide[field, at_y, 10:14, :] = value[0:4]

    for f in range(6):
        place(f, 1, 0, co[f])
    place(6, 1, 0, cs[...])
    for copy in coarse_c:
        copy.wait_recv()
    for k, (dx, dy) in enumerate(NEIGHBOURS):
        for f in range(6):
            place(f, dy + 1, dx, got_co[k, f])
    cc = [wide[f] for f in range(6)]
    spacing = 1.0 / 16.0
    coarse_w = DAMP / (-2.0 * spacing * (cc[0] + cc[1] + cc[2]) - SCREEN)
    cc = [spacing * c for c in cc]
    for copy in coarse_s:
        copy.wait_recv()
    for k, (dx, dy) in enumerate(NEIGHBOURS):
        place(6, dy + 1, dx, got_cs[k])
    coarse_b = wide[6]
    lane = lax.broadcasted_iota(jnp.int32, (3, 16, nz), 2)
    in_group = lane % group

    def y_up(v):
        r = pltpu.roll(v, nz - group, 2)
        return jnp.where(lane < nz - group, r, jnp.concatenate([r[1:], r[:1]], axis=0))

    def y_down(v):
        r = pltpu.roll(v, group, 2)
        return jnp.where(lane >= group, r, jnp.concatenate([r[2:], r[:2]], axis=0))

    value = coarse_w * coarse_b
    for _ in range(3):
        zp = jnp.where(in_group == group - 1, pltpu.roll(value, group - 1, 2), pltpu.roll(value, nz - 1, 2))
        zm = jnp.where(in_group == 0, pltpu.roll(value, nz - group + 1, 2), pltpu.roll(value, 1, 2))
        dz = zp - zm
        yp, ym = y_up(value), y_down(value)
        dy_ = yp - ym
        xs = pltpu.roll(value, 15, 1) + pltpu.roll(value, 1, 1)
        dxy = pltpu.roll(dy_, 15, 1) - pltpu.roll(dy_, 1, 1)
        dxz = pltpu.roll(dz, 15, 1) - pltpu.roll(dz, 1, 1)
        dyz = y_up(dz) - y_down(dz)
        total = cc[0] * xs + cc[1] * (yp + ym) + cc[2] * (zp + zm)
        total = total + (cc[3] * dxy + cc[4] * dxz + cc[5] * dyz)
        value = (1.0 - DAMP) * value + coarse_w * (coarse_b - total)

    rows_b = lax.broadcasted_iota(jnp.int32, (nz, nz), 0)
    cols_b = lax.broadcasted_iota(jnp.int32, (nz, nz), 1)
    for j, (blk, g) in enumerate(((0, 3), (1, 0), (1, 1), (1, 2), (1, 3), (2, 0))):
        table = jnp.where(rows_b == g * group + cols_b // 4, 1.0, 0.0).astype(jnp.bfloat16)
        grown[j] = dot_exact(value[blk], table)

    for copy in round_2:
        copy.wait_recv()

    def row(j, i):
        return jnp.broadcast_to(grown[j, 3 + i : 4 + i, :], (8, nz))

    for i in range(nx // 4 + 2):
        a0 = jnp.where(sub < 4, row(1, i), row(2, i))
        a1 = jnp.where(sub < 4, row(3, i), row(4, i))
        a2 = jnp.where(sub < 4, row(5, i), row(0, i))
        for at in range(4 * i, 4 * i + 4):
            if 1 <= at < x1 + 3:
                base = two if x0 <= at < x1 else fin
                fin[at, 0:8] = base[at, 0:8] + a0
                fin[at, 8:16] = base[at, 8:16] + a1
                fin[at, 16:24] = jnp.where(sub < 4, est_hi[at], est_lo[at]) + a2

    sweep(fin, one, x0 - 2, x1 + 2)
    for copy in round_2:
        copy.wait_send()
    sweep(one, two, x0 - 1, x1 + 1)

    def emit_last(at, v, *terms):
        up_out[at - x0] = v[0:ny]
        res_out[at - x0] = residual_at(at, v, *terms)

    walk(two, x0, x1, emit_last)
    for copy in round_1 + coarse_c + coarse_s:
        copy.wait_send()


def solution(mesh):
    gx_n, gy_n = mesh.shape["gx"], mesh.shape["gy"]

    def shards(potential, density, correction):
        nx, ny, nz = potential.shape
        fine = pltpu.VMEM((nx + 8, ny + 8, nz), F32)
        side = pltpu.VMEM((nx + 8, 8, nz), F32)
        dma = pltpu.SemaphoreType.DMA
        shape = jax.ShapeDtypeStruct(potential.shape, F32)
        return pl.pallas_call(
            functools.partial(kernel, gx_n, gy_n),
            out_shape=(shape, shape),
            in_specs=[pl.BlockSpec(memory_space=pl.ANY)] * 3,
            out_specs=[pl.BlockSpec(memory_space=pltpu.VMEM)] * 2,
            scratch_shapes=[
                fine, fine, fine,
                pltpu.VMEM((6, nx + 8, ny + 8, nz), F32),
                fine, fine, fine, fine, fine,
                pltpu.VMEM((nx, 8, nz), F32), pltpu.VMEM((nx, 8, nz), F32),
                side, side, side, side,
                pltpu.VMEM((48 * ny, nz), F32), pltpu.VMEM((8 * ny, nz), F32),
                pltpu.VMEM((6, 8, nz), F32), pltpu.VMEM((8, nz), F32),
                pltpu.VMEM((8, 6, 8, nz), F32), pltpu.VMEM((8, 8, nz), F32),
                pltpu.VMEM((7, 3, 16, nz), F32), pltpu.VMEM((6, 16, nz), F32),
                dma((3,)), dma((12,)), dma((12,)), dma((8,)), dma((8,)),
                dma((8,)), dma((8,)), dma((8,)), dma((8,)),
            ],
            compiler_params=pltpu.CompilerParams(
                collective_id=0, has_side_effects=True, vmem_limit_bytes=40 * 1024 * 1024
            ),
        )(potential, density, correction)

    placed = (P("gx", "gy", None),) * 3
    return jax.shard_map(
        shards, mesh=mesh, in_specs=placed,
        out_specs=(P("gx", "gy", None), P("gx", "gy", None)), check_vma=False,
    )
```

time: 118 us -> 33.3 us (0.28)
  waiting for transfers between devices: 61.1 us -> 0 us
  starting transfers between devices: 33.9 us -> 0 us
  Pallas kernels: 0 us -> 28.4 us
  other arithmetic: 10.3 us -> 0 us
  local copies, waits for them, and re-layouts: 9.42 us -> 4.13 us
  matrix products: 1.92 us -> 0 us
    ppermute x40 -> x0, waiting for transfers between devices: 61.1 us -> none  [the longest x20 46.6 us: extended_2(): lax.ppermute(tail, axis, [(i, (i + 1) % count) for i in range(count)])]
    ppermute x40 -> x0, starting transfers between devices: 33.9 us -> none  [the longest x20 17.8 us: extended_2(): lax.ppermute(tail, axis, [(i, (i + 1) % count) for i in range(count)])]
    pallas_call x0 -> x1, Pallas kernels: none -> 28.4 us  [shards(): pl.pallas_call(functools.partial(kernel, gx_n, gy_n), out_shape=(shape, s...]
    slice x54 -> x0, local copies, waits for them, and re-layouts: 6.99 us -> none  [the longest x42 5.49 us: getter(): return jnp.roll(window, -shift_z, axis=2)]
    add x8 -> x0, other arithmetic: 3.82 us -> none  [the longest x6 3.5 us: relax_padded(): centre + damping * (source - operate(cropper(padded), coeffs, spacing)) /...]
    concatenate x24 -> x0, other arithmetic: 3.56 us -> none  [extended_2(): jnp.concatenate([lax.ppermute(tail, axis, [(i, (i + 1) % count) for i in...]
    unnamed x12 -> x8, local copies, waits for them, and re-layouts: 1.53 us -> 4.13 us
    sub x2 -> x0, other arithmetic: 1.94 us -> none  [the longest x1 1.31 us: shards(): residual = source - operate(cropper(rim_one(estimate)), coeffs, 1.0)]
  transfers between devices with their start and end apart: 40 -> 0, of which waited for: 34 -> 0; matrix products, arithmetic and copies ran while one was open for 7% -> 0% of each run, Pallas kernels for 0% -> 0%
where the time goes in v1:
time: 33.3 us; the launch traced here: 33.2 us
  Pallas kernels  28.4 us (85%)
  local copies, waits for them, and re-layouts  4.13 us (12%)
  between operations  0.65 us (2%)
    pallas_call x1, Pallas kernels, shards(): pl.pallas_call(functools.partial(kernel, gx_n, gy_n), out_shape=(shape, s...  28.4 us
    unnamed x8, local copies, waits for them, and re-layouts  4.13 us

profile of v1, /device:TPU:0, one launch (start us, length us, event | category | flops | bytes accessed | tf_op | source)
XLA Modules:
  0.0 33.2 jit_solution(1998210686253165390)
XLA Ops:
  0.6 0.0 copy-start
  0.6 0.9 %copy-done = f32[24,16,128]{2,1,0:T(8,128)S(1)} copy-done((f32[24,16,128]{2,1,0:T(8,128)S(1)}, f32[24,16,128]{2,1,0:T(8,128)}, u32[]{:S(2)}) %copy-start) | copy-done | bytes 196632
  1.6 0.0 copy-start.1
  1.6 0.9 %copy-done.1 = f32[24,16,128]{2,1,0:T(8,128)S(1)} copy-done((f32[24,16,128]{2,1,0:T(8,128)S(1)}, f32[24,16,128]{2,1,0:T(8,128)}, u32[]{:S(2)}) %copy-start.1) | copy-done | bytes 196632
  2.5 0.0 copy-start.2
  2.5 0.9 %copy-done.2 = f32[24,16,128]{2,1,0:T(8,128)S(1)} copy-done((f32[24,16,128]{2,1,0:T(8,128)S(1)}, f32[24,16,128]{2,1,0:T(8,128)}, u32[]{:S(2)}) %copy-start.2) | copy-done | bytes 196632
  3.4 28.4 %shard_map.50 = (f32[24,16,128]{2,1,0:T(8,128)S(1)}, f32[24,16,128]{2,1,0:T(8,128)S(1)}) custom-call(f32[24,16,128]{2,1,0:T(8,128)S(1)} %copy-done, f32[24,16,128]{2,1,0:T(8,128)S(1)} %copy-done.1, f32[24,16,128]{2,1,0:T(8,128)S(1)} %copy-done.2), custom_call_target="tpu_custom_call" | custom-call | tf_op jit(solution)/shard_map/pallas_call | solution.py:336
  31.8 0.7 %copy.7 = f32[24,16,128]{2,1,0:T(8,128)} copy(f32[24,16,128]{2,1,0:T(8,128)S(1)} %get-tuple-element.4) | data formatting | bytes 393216
  32.5 0.7 %copy.8 = f32[24,16,128]{2,1,0:T(8,128)} copy(f32[24,16,128]{2,1,0:T(8,128)S(1)} %get-tuple-element.5) | data formatting | bytes 393216
Async XLA Ops:
  0.6 0.9 %copy-start = (f32[24,16,128]{2,1,0:T(8,128)S(1)}, f32[24,16,128]{2,1,0:T(8,128)}, u32[]{:S(2)}) copy-start(f32[24,16,128]{2,1,0:T(8,128)} %p_in.1) | copy-start | bytes 589828
  1.6 0.9 %copy-start.1 = (f32[24,16,128]{2,1,0:T(8,128)S(1)}, f32[24,16,128]{2,1,0:T(8,128)}, u32[]{:S(2)}) copy-start(f32[24,16,128]{2,1,0:T(8,128)} %d_in.1) | copy-start | bytes 589828
  2.5 0.9 %copy-start.2 = (f32[24,16,128]{2,1,0:T(8,128)S(1)}, f32[24,16,128]{2,1,0:T(8,128)}, u32[]{:S(2)}) copy-start(f32[24,16,128]{2,1,0:T(8,128)} %c_in.1) | copy-start | bytes 589828

commit v2 on v1

--- a/solution.py
+++ b/solution.py
@@ -26,7 +26,7 @@
     return v, dz, yp - ym, zp + zm, yp + ym, dyz
 
 
-def walk(ref, low, high, emit, unroll=2):
+def walk(ref, low, high, emit):
     def step(at, carry):
         before, here = carry
         after = first_plane(ref, at + 1)
@@ -43,7 +43,7 @@
         return here[:3], after
 
     start = (first_plane(ref, low - 1)[:3], first_plane(ref, low))
-    lax.fori_loop(low, high, step, start, unroll=unroll)
+    lax.fori_loop(low, high, step, start, unroll=8 if (high - low) % 8 == 0 else 7)
 
 
 def dot_exact(values, table):
@@ -59,8 +59,8 @@
 def kernel(
     gx_n, gy_n, p_in, d_in, c_in, up_out, res_out,
     pot, cor, den, coef, wgt, src, one, two, fin,
-    msg_lo, msg_hi, got_lo, got_hi, est_lo, est_hi,
-    pool_c, pool_s, co, cs, got_co, got_cs, wide, grown,
+    msg_lo, msg_hi, got_lo, got_hi, out_lo, out_hi, est_lo, est_hi,
+    pool_c, pool_s, co, co_lo, co_hi, cs, got_co, got_cox, got_cs, wide, grown,
     in_sem, s1, r1, s2, r2, sc, rc, ss, rs,
 ):
     nx, ny, nz = p_in.shape
@@ -71,15 +71,14 @@
     def device(dx, dy):
         return (lax.rem(gx + dx + gx_n, gx_n), lax.rem(gy + dy + gy_n, gy_n))
 
+    barrier = pltpu.get_barrier_semaphore()
+    for dx, dy in sorted(NEIGHBOURS, key=lambda d: -2 * abs(d[0]) - abs(d[1])):
+        pl.semaphore_signal(barrier, inc=1, device_id=device(dx, dy), device_id_type=MESH)
     loads = []
     for k, (a, b) in enumerate(((p_in, pot), (c_in, cor), (d_in, den))):
         copy = pltpu.make_async_copy(a, b.at[x0:x1, 0:ny], in_sem.at[k])
         copy.start()
         loads.append(copy)
-    barrier = pltpu.get_barrier_semaphore()
-    for dx, dy in NEIGHBOURS:
-        pl.semaphore_signal(barrier, inc=1, device_id=device(dx, dy), device_id_type=MESH)
-
     sub = lax.broadcasted_iota(jnp.int32, (8, nz), 0)
     wide[:, :, 14:16, :] = jnp.zeros((7, 3, 2, nz), F32)
     for f in range(6):
@@ -112,12 +111,16 @@
         copy.start()
         return copy
 
-    def y_sends(low, high, into_low, into_high, send, recv, k):
+    def y_sends(low, high, into_low, into_high, send, recv, k, width, count, head):
         out = []
+        tail = head + count
         for dy, part, into in ((1, low, into_low), (-1, high, into_high)):
-            out.append(remote(part(0, nx), into.at[x0:x1], send, recv, k, device(0, dy)))
-            out.append(remote(part(0, 3), into.at[x1 : x1 + 3], send, recv, k + 1, device(-1, dy)))
-            out.append(remote(part(nx - 3, nx), into.at[1:x0], send, recv, k + 2, device(1, dy)))
+            out.append(remote(
+                part.at[0:width], into.at[tail : tail + width], send, recv, k, device(-1, dy)))
+            out.append(remote(
+                part.at[count - width : count], into.at[head - width : head],
+                send, recv, k + 1, device(1, dy)))
+            out.append(remote(part, into.at[head:tail], send, recv, k + 2, device(0, dy)))
             k += 3
         return out
 
@@ -129,8 +132,7 @@
         round_1.append(remote(
             ref.at[x0 : x0 + width, 0:ny], ref.at[x1 : x1 + width, 0:ny], s1, r1, k + 1, device(-1, 0)))
         k += 2
-    round_1 += y_sends(
-        lambda a, b: msg_lo.at[a:b], lambda a, b: msg_hi.at[a:b], got_lo, got_hi, s1, r1, k)
+    round_1 += y_sends(msg_lo, msg_hi, got_lo, got_hi, s1, r1, k, 3, nx, x0)
 
     rows_at = lax.broadcasted_iota(jnp.int32, (4 * nz, nz), 0)
     cols_at = lax.broadcasted_iota(jnp.int32, (4 * nz, nz), 1)
@@ -187,9 +189,18 @@
 
     lax.fori_loop(0, nx // 4, pool_coef, 0)
     co[...] = pooled(pool_c, 48).reshape(6, 8, nz)
-    coarse_c = [
-        remote(co, got_co.at[7 - k], sc, rc, k, device(*NEIGHBOURS[k])) for k in range(8)
-    ]
+    for p in range(3):
+        f, g = co[2 * p], co[2 * p + 1]
+        co_lo[p] = jnp.where(sub < 4, pltpu.roll(f, 6, 0), pltpu.roll(g, 2, 0))
+        co_hi[p] = jnp.where(sub < 4, f, pltpu.roll(g, 4, 0))
+    coarse_c = []
+    for k in (1, 6, 0, 2, 5, 7, 3, 4):
+        dx = NEIGHBOURS[k][0]
+        if dx == 0:
+            a, b = co, got_co.at[(7 - k) - 3]
+        else:
+            a, b = (co_lo if dx > 0 else co_hi), got_cox.at[7 - k]
+        coarse_c.append(remote(a, b, sc, rc, k, device(*NEIGHBOURS[k])))
 
     def off_diagonal(at, xs, ys, zs, dxy, dxz, dyz):
         return (
@@ -218,10 +229,12 @@
     round_2 = [
         remote(two.at[x1 - 3 : x1, 0:ny], fin.at[1:x0, 0:ny], s2, r2, 0, device(1, 0)),
         remote(two.at[x0 : x0 + 3, 0:ny], fin.at[x1 : x1 + 3, 0:ny], s2, r2, 1, device(-1, 0)),
-    ] + y_sends(
-        lambda a, b: two.at[x0 + a : x0 + b, ny - 8 : ny],
-        lambda a, b: two.at[x0 + a : x0 + b, 0:8],
-        est_lo, est_hi, s2, r2, 2)
+    ]
+    for q in range(nx // 2):
+        a, b = x0 + 2 * q, x0 + 2 * q + 1
+        out_lo[q] = jnp.where(sub < 4, pltpu.roll(two[a, ny - 8 : ny], 4, 0), two[b, ny - 8 : ny])
+        out_hi[q] = jnp.where(sub < 4, two[a, 0:8], pltpu.roll(two[b, 0:8], 4, 0))
+    round_2 += y_sends(out_lo, out_hi, est_lo, est_hi, s2, r2, 2, 2, nx // 2, x0 // 2)
 
     def emit_first(at, v, *terms):
         res_out[at - x0] = residual_at(at, v, *terms)
@@ -251,7 +264,11 @@
         copy.wait_recv()
     for k, (dx, dy) in enumerate(NEIGHBOURS):
         for f in range(6):
-            place(f, dy + 1, dx, got_co[k, f])
+            if dx == 0:
+                place(f, dy + 1, 0, got_co[k - 3, f])
+            else:
+                row_at, part = (0 if dx < 0 else 10), 4 * (f % 2)
+                wide[f, dy + 1, row_at : row_at + 4, :] = got_cox[k, f // 2, part : part + 4]
     cc = [wide[f] for f in range(6)]
     spacing = 1.0 / 16.0
     coarse_w = DAMP / (-2.0 * spacing * (cc[0] + cc[1] + cc[2]) - SCREEN)
@@ -308,7 +325,12 @@
                 base = two if x0 <= at < x1 else fin
                 fin[at, 0:8] = base[at, 0:8] + a0
                 fin[at, 8:16] = base[at, 8:16] + a1
-                fin[at, 16:24] = jnp.where(sub < 4, est_hi[at], est_lo[at]) + a2
+                lo, hi = est_lo[at // 2], est_hi[at // 2]
+                if at % 2 == 0:
+                    lo = pltpu.roll(lo, 4, 0)
+                else:
+                    hi = pltpu.roll(hi, 4, 0)
+                fin[at, ny : ny + 8] = jnp.where(sub < 4, hi, lo) + a2
 
     sweep(fin, one, x0 - 2, x1 + 2)
     for copy in round_2:
@@ -331,6 +353,8 @@
         nx, ny, nz = potential.shape
         fine = pltpu.VMEM((nx + 8, ny + 8, nz), F32)
         side = pltpu.VMEM((nx + 8, 8, nz), F32)
+        half_out = pltpu.VMEM((nx // 2, 8, nz), F32)
+        half = pltpu.VMEM((nx // 2 + 4, 8, nz), F32)
         dma = pltpu.SemaphoreType.DMA
         shape = jax.ShapeDtypeStruct(potential.shape, F32)
         return pl.pallas_call(
@@ -343,10 +367,11 @@
                 pltpu.VMEM((6, nx + 8, ny + 8, nz), F32),
                 fine, fine, fine, fine, fine,
                 pltpu.VMEM((nx, 8, nz), F32), pltpu.VMEM((nx, 8, nz), F32),
-                side, side, side, side,
+                side, side, half_out, half_out, half, half,
                 pltpu.VMEM((48 * ny, nz), F32), pltpu.VMEM((8 * ny, nz), F32),
-                pltpu.VMEM((6, 8, nz), F32), pltpu.VMEM((8, nz), F32),
-                pltpu.VMEM((8, 6, 8, nz), F32), pltpu.VMEM((8, 8, nz), F32),
+                pltpu.VMEM((6, 8, nz), F32), pltpu.VMEM((3, 8, nz), F32), pltpu.VMEM((3, 8, nz), F32),
+                pltpu.VMEM((8, nz), F32),
+                pltpu.VMEM((2, 6, 8, nz), F32), pltpu.VMEM((8, 3, 8, nz), F32), pltpu.VMEM((8, 8, nz), F32),
                 pltpu.VMEM((7, 3, 16, nz), F32), pltpu.VMEM((6, 16, nz), F32),
                 dma((3,)), dma((12,)), dma((12,)), dma((8,)), dma((8,)),
                 dma((8,)), dma((8,)), dma((8,)), dma((8,)),
@@ -354,7 +379,9 @@
             compiler_params=pltpu.CompilerParams(
                 collective_id=0, has_side_effects=True, vmem_limit_bytes=40 * 1024 * 1024
             ),
-        )(potential, density, correction)
+        )(*[
+            pltpu.with_memory_space_constraint(v, pltpu.HBM) for v in (potential, density, correction)
+        ])
 
     placed = (P("gx", "gy", None),) * 3
     return jax.shard_map(

time: 33.3 us -> 25.2 us (0.76)
  Pallas kernels: 28.4 us -> 23 us
  local copies, waits for them, and re-layouts: 4.13 us -> 1.36 us
    pallas_call x1, Pallas kernels: 28.4 us -> 23 us  [shards(): pl.pallas_call(functools.partial(kernel, gx_n, gy_n), out_shape=(shape, s...]
    unnamed x8 -> x2, local copies, waits for them, and re-layouts: 4.13 us -> 1.36 us
where the time goes in v2:
time: 25.2 us; the launch traced here: 25 us
  Pallas kernels  23 us (91%)
  local copies, waits for them, and re-layouts  1.36 us (5%)
  between operations  0.64 us (3%)
    pallas_call x1, Pallas kernels, shards(): pl.pallas_call(functools.partial(kernel, gx_n, gy_n), out_shape=(shape, s...  23 us
    unnamed x2, local copies, waits for them, and re-layouts  1.36 us

profile of v2, /device:TPU:0, one launch (start us, length us, event | category | flops | bytes accessed | tf_op | source)
XLA Modules:
  0.0 25.0 jit_solution(8661538171320050392)
XLA Ops:
  0.6 23.0 %shard_map.50 = (f32[24,16,128]{2,1,0:T(8,128)S(1)}, f32[24,16,128]{2,1,0:T(8,128)S(1)}) custom-call(f32[24,16,128]{2,1,0:T(8,128)} %p_in.1, f32[24,16,128]{2,1,0:T(8,128)} %d_in.1, f32[24,16,128]{2,1,0:T(8,128)} %c_in.1), custom_call_target="tpu_custom_call" | custom-call | tf_op jit(solution)/shard_map/pallas_call | solution.py:360
  23.7 0.7 %copy.7 = f32[24,16,128]{2,1,0:T(8,128)} copy(f32[24,16,128]{2,1,0:T(8,128)S(1)} %get-tuple-element.4) | data formatting | bytes 393216
  24.4 0.7 %copy.8 = f32[24,16,128]{2,1,0:T(8,128)} copy(f32[24,16,128]{2,1,0:T(8,128)S(1)} %get-tuple-element.5) | data formatting | bytes 393216

commit v3 on v2

--- a/solution.py
+++ b/solution.py
@@ -10,7 +10,9 @@
 MESH = pl.DeviceIdType.MESH
 SCREEN = 0.002
 DAMP = 0.6
+UNROLL = {3: 3, 4: 4, 20: 10, 22: 11, 24: 8}
 F32 = jnp.float32
+BESIDE = [(-1, 0), (1, 0), (0, -1), (0, 1)]
 NEIGHBOURS = [(-1, -1), (-1, 0), (-1, 1), (0, -1), (0, 1), (1, -1), (1, 0), (1, 1)]
 
 
@@ -43,7 +45,7 @@
         return here[:3], after
 
     start = (first_plane(ref, low - 1)[:3], first_plane(ref, low))
-    lax.fori_loop(low, high, step, start, unroll=8 if (high - low) % 8 == 0 else 7)
+    lax.fori_loop(low, high, step, start, unroll=UNROLL.get(high - low, 7))
 
 
 def dot_exact(values, table):
@@ -72,7 +74,7 @@
         return (lax.rem(gx + dx + gx_n, gx_n), lax.rem(gy + dy + gy_n, gy_n))
 
     barrier = pltpu.get_barrier_semaphore()
-    for dx, dy in sorted(NEIGHBOURS, key=lambda d: -2 * abs(d[0]) - abs(d[1])):
+    for dx, dy in BESIDE:
         pl.semaphore_signal(barrier, inc=1, device_id=device(dx, dy), device_id_type=MESH)
     loads = []
     for k, (a, b) in enumerate(((p_in, pot), (c_in, cor), (d_in, den))):
@@ -101,7 +103,7 @@
         return 0
 
     lax.fori_loop(0, nx, pack, 0, unroll=4)
-    pl.semaphore_wait(barrier, 8)
+    pl.semaphore_wait(barrier, 4)
 
     def remote(a, b, send, recv, k, to):
         copy = pltpu.make_async_remote_copy(
@@ -124,15 +126,18 @@
             k += 3
         return out
 
-    round_1 = []
-    k = 0
+    got = ((got_lo, msg_lo, 1), (got_hi, msg_hi, -1))
+    beside_y = [
+        remote(msg, into.at[x0:x1], s1, r1, k, device(0, dy)) for k, (into, msg, dy) in enumerate(got)
+    ]
+    beside_x = []
+    k = 2
     for ref, width in ((pot, 3), (cor, 3), (den, 2)):
-        round_1.append(remote(
+        beside_x.append(remote(
             ref.at[x1 - width : x1, 0:ny], ref.at[x0 - width : x0, 0:ny], s1, r1, k, device(1, 0)))
-        round_1.append(remote(
+        beside_x.append(remote(
             ref.at[x0 : x0 + width, 0:ny], ref.at[x1 : x1 + width, 0:ny], s1, r1, k + 1, device(-1, 0)))
         k += 2
-    round_1 += y_sends(msg_lo, msg_hi, got_lo, got_hi, s1, r1, k, 3, nx, x0)
 
     rows_at = lax.broadcasted_iota(jnp.int32, (4 * nz, nz), 0)
     cols_at = lax.broadcasted_iota(jnp.int32, (4 * nz, nz), 1)
@@ -150,8 +155,15 @@
             parts.append(total)
         return dot_exact(jnp.concatenate(parts, axis=1), mean_table)
 
-    for copy in round_1:
+    for copy in beside_y:
         copy.wait_recv()
+    for into in (got_lo, got_hi):
+        beside_x.append(remote(
+            into.at[x1 - 3 : x1], into.at[1:x0], s1, r1, k, device(1, 0)))
+        beside_x.append(remote(
+            into.at[x0 : x0 + 3], into.at[x1 : x1 + 3], s1, r1, k + 1, device(-1, 0)))
+        k += 2
+    round_1 = beside_y + beside_x
 
     def unpack(at, _):
         lo, hi = got_lo[at], got_hi[at]
@@ -160,7 +172,7 @@
         den[at, ny : ny + 8] = jnp.where(sub < 4, pltpu.roll(hi, 2, 0), pltpu.roll(lo, 6, 0))
         return 0
 
-    lax.fori_loop(1, x1 + 3, unpack, 0, unroll=3)
+    lax.fori_loop(x0, x1, unpack, 0, unroll=4)
 
     def build(at, v, xs, ys, zs, dxy, dxz, dyz):
         twice = 2.0 * v
@@ -177,7 +189,26 @@
         coef[0, at], coef[1, at], coef[2, at] = cxx, cyy, czz
         coef[3, at], coef[4, at], coef[5, at] = 0.5 * cxy, 0.5 * cxz, 0.5 * cyz
 
-    walk(pot, x0 - 2, x1 + 2, build)
+    def off_diagonal(at, xs, ys, zs, dxy, dxz, dyz):
+        return (
+            (coef[0, at] * xs + coef[1, at] * ys + coef[2, at] * zs)
+            + (coef[3, at] * dxy + coef[4, at] * dxz + coef[5, at] * dyz)
+        )
+
+    def sweep(a, b, low, high):
+        def emit(at, v, *terms):
+            b[at] = (1.0 - DAMP) * v + wgt[at] * (src[at] - off_diagonal(at, *terms))
+
+        walk(a, low, high, emit)
+
+    walk(pot, x0 + 1, x1 - 1, build)
+    sweep(cor, one, x0 + 2, x1 - 2)
+    for copy in beside_x:
+        copy.wait_recv()
+    lax.fori_loop(1, x0, unpack, 0, unroll=3)
+    lax.fori_loop(x1, x1 + 3, unpack, 0, unroll=3)
+    walk(pot, x0 - 2, x0 + 1, build)
+    walk(pot, x1 - 1, x1 + 2, build)
 
     def pool_coef(i, _):
         for f in range(6):
@@ -202,18 +233,6 @@
             a, b = (co_lo if dx > 0 else co_hi), got_cox.at[7 - k]
         coarse_c.append(remote(a, b, sc, rc, k, device(*NEIGHBOURS[k])))
 
-    def off_diagonal(at, xs, ys, zs, dxy, dxz, dyz):
-        return (
-            (coef[0, at] * xs + coef[1, at] * ys + coef[2, at] * zs)
-            + (coef[3, at] * dxy + coef[4, at] * dxz + coef[5, at] * dyz)
-        )
-
-    def sweep(a, b, low, high):
-        def emit(at, v, *terms):
-            b[at] = (1.0 - DAMP) * v + wgt[at] * (src[at] - off_diagonal(at, *terms))
-
-        walk(a, low, high, emit)
-
     def residual_at(at, v, *terms):
         n = ny
         cut = [t[0:n] for t in terms]
@@ -223,7 +242,8 @@
         total = total + (c[3] * cut[3] + c[4] * cut[4] + c[5] * cut[5])
         return src[at, 0:n] - (total + main * v[0:n])
 
-    sweep(cor, one, x0 - 2, x1 + 2)
+    sweep(cor, one, x0 - 2, x0 + 2)
+    sweep(cor, one, x1 - 2, x1 + 2)
     sweep(one, two, x0 - 1, x1 + 1)
 
     round_2 = [

time: 25.2 us -> 24.3 us (0.964)
  Pallas kernels: 23 us -> 22.1 us
    pallas_call x1, Pallas kernels: 23 us -> 22.1 us  [shards(): pl.pallas_call(functools.partial(kernel, gx_n, gy_n), out_shape=(shape, s...]
where the time goes in v3:
time: 24.3 us; the launch traced here: 24.1 us
  Pallas kernels  22.1 us (91%)
  local copies, waits for them, and re-layouts  1.36 us (6%)
  between operations  0.64 us (3%)
    pallas_call x1, Pallas kernels, shards(): pl.pallas_call(functools.partial(kernel, gx_n, gy_n), out_shape=(shape, s...  22.1 us
    unnamed x2, local copies, waits for them, and re-layouts  1.36 us

profile of v3, /device:TPU:0, one launch (start us, length us, event | category | flops | bytes accessed | tf_op | source)
XLA Modules:
  0.0 24.1 jit_solution(2762178904892414400)
XLA Ops:
  0.6 22.1 %shard_map.50 = (f32[24,16,128]{2,1,0:T(8,128)S(1)}, f32[24,16,128]{2,1,0:T(8,128)S(1)}) custom-call(f32[24,16,128]{2,1,0:T(8,128)} %p_in.1, f32[24,16,128]{2,1,0:T(8,128)} %d_in.1, f32[24,16,128]{2,1,0:T(8,128)} %c_in.1), custom_call_target="tpu_custom_call" | custom-call | tf_op jit(solution)/shard_map/pallas_call | solution.py:380
  22.8 0.7 %copy.7 = f32[24,16,128]{2,1,0:T(8,128)} copy(f32[24,16,128]{2,1,0:T(8,128)S(1)} %get-tuple-element.4) | data formatting | bytes 393216
  23.4 0.7 %copy.8 = f32[24,16,128]{2,1,0:T(8,128)} copy(f32[24,16,128]{2,1,0:T(8,128)S(1)} %get-tuple-element.5) | data formatting | bytes 393216

commit v4 on v3

--- a/solution.py
+++ b/solution.py
@@ -10,7 +10,7 @@
 MESH = pl.DeviceIdType.MESH
 SCREEN = 0.002
 DAMP = 0.6
-UNROLL = {3: 3, 4: 4, 20: 10, 22: 11, 24: 8}
+UNROLL = {3: 3, 4: 4, 20: 10, 22: 11, 24: 12, 26: 13, 28: 14}
 F32 = jnp.float32
 BESIDE = [(-1, 0), (1, 0), (0, -1), (0, 1)]
 NEIGHBOURS = [(-1, -1), (-1, 0), (-1, 1), (0, -1), (0, 1), (1, -1), (1, 0), (1, 1)]
@@ -62,7 +62,7 @@
     gx_n, gy_n, p_in, d_in, c_in, up_out, res_out,
     pot, cor, den, coef, wgt, src, one, two, fin,
     msg_lo, msg_hi, got_lo, got_hi, out_lo, out_hi, est_lo, est_hi,
-    pool_c, pool_s, co, co_lo, co_hi, cs, got_co, got_cox, got_cs, wide, grown,
+    pool_c, pool_s, co, co_lo, co_hi, cs, got_co, got_cox, got_cs, wide, grown, back,
     in_sem, s1, r1, s2, r2, sc, rc, ss, rs,
 ):
     nx, ny, nz = p_in.shape
@@ -201,8 +201,18 @@
 
         walk(a, low, high, emit)
 
+    def pool_coef(i, _):
+        for f in range(6):
+            total = coef[f, x0 + 4 * i, 0:ny]
+            for j in range(1, 4):
+                total = total + coef[f, x0 + 4 * i + j, 0:ny]
+            at = (f * 8 + i) * ny
+            pool_c[pl.ds(at if isinstance(i, int) else pl.multiple_of(at, 8), ny), :] = total
+        return 0
+
     walk(pot, x0 + 1, x1 - 1, build)
     sweep(cor, one, x0 + 2, x1 - 2)
+    lax.fori_loop(1, nx // 4 - 1, pool_coef, 0, unroll=2)
     for copy in beside_x:
         copy.wait_recv()
     lax.fori_loop(1, x0, unpack, 0, unroll=3)
@@ -210,15 +220,8 @@
     walk(pot, x0 - 2, x0 + 1, build)
     walk(pot, x1 - 1, x1 + 2, build)
 
-    def pool_coef(i, _):
-        for f in range(6):
-            total = coef[f, x0 + 4 * i, 0:ny]
-            for j in range(1, 4):
-                total = total + coef[f, x0 + 4 * i + j, 0:ny]
-            pool_c[pl.ds(pl.multiple_of((f * 8 + i) * ny, 8), ny), :] = total
-        return 0
-
-    lax.fori_loop(0, nx // 4, pool_coef, 0)
+    pool_coef(0, 0)
+    pool_coef(nx // 4 - 1, 0)
     co[...] = pooled(pool_c, 48).reshape(6, 8, nz)
     for p in range(3):
         f, g = co[2 * p], co[2 * p + 1]
@@ -246,6 +249,20 @@
     sweep(cor, one, x1 - 2, x1 + 2)
     sweep(one, two, x0 - 1, x1 + 1)
 
+    def emit_first(at, v, *terms):
+        res_out[at - x0] = residual_at(at, v, *terms)
+
+    walk(two, x0, x1, emit_first)
+    for i in range(nx // 4):
+        pool_s[i * ny : (i + 1) * ny, :] = (
+            (res_out[4 * i] + res_out[4 * i + 1]) + (res_out[4 * i + 2] + res_out[4 * i + 3])
+        )
+    cs[...] = pooled(pool_s, 8)
+    coarse_s = [
+        remote(cs, got_cs.at[7 - k], ss, rs, k, device(*NEIGHBOURS[k]))
+        for k in (0, 2, 5, 7, 1, 6, 3, 4)
+    ]
+
     round_2 = [
         remote(two.at[x1 - 3 : x1, 0:ny], fin.at[1:x0, 0:ny], s2, r2, 0, device(1, 0)),
         remote(two.at[x0 : x0 + 3, 0:ny], fin.at[x1 : x1 + 3, 0:ny], s2, r2, 1, device(-1, 0)),
@@ -256,19 +273,6 @@
         out_hi[q] = jnp.where(sub < 4, two[a, 0:8], pltpu.roll(two[b, 0:8], 4, 0))
     round_2 += y_sends(out_lo, out_hi, est_lo, est_hi, s2, r2, 2, 2, nx // 2, x0 // 2)
 
-    def emit_first(at, v, *terms):
-        res_out[at - x0] = residual_at(at, v, *terms)
-
-    walk(two, x0, x1, emit_first)
-    for i in range(nx // 4):
-        pool_s[i * ny : (i + 1) * ny, :] = (
-            (res_out[4 * i] + res_out[4 * i + 1]) + (res_out[4 * i + 2] + res_out[4 * i + 3])
-        )
-    cs[...] = pooled(pool_s, 8)
-    coarse_s = [
-        remote(cs, got_cs.at[7 - k], ss, rs, k, device(*NEIGHBOURS[k])) for k in range(8)
-    ]
-
     def place(field, at_y, dx, value):
         if dx < 0:
             wide[field, at_y, 0:4, :] = value[2:6]
@@ -277,6 +281,10 @@
         else:
             wide[field, at_y, 10:14, :] = value[0:4]
 
+    rows_b = lax.broadcasted_iota(jnp.int32, (nz, nz), 0)
+    cols_b = lax.broadcasted_iota(jnp.int32, (nz, nz), 1)
+    for g in range(4):
+        back[g] = jnp.where(rows_b == g * group + cols_b // 4, 1.0, 0.0).astype(jnp.bfloat16)
     for f in range(6):
         place(f, 1, 0, co[f])
     place(6, 1, 0, cs[...])
@@ -324,11 +332,8 @@
         total = total + (cc[3] * dxy + cc[4] * dxz + cc[5] * dyz)
         value = (1.0 - DAMP) * value + coarse_w * (coarse_b - total)
 
-    rows_b = lax.broadcasted_iota(jnp.int32, (nz, nz), 0)
-    cols_b = lax.broadcasted_iota(jnp.int32, (nz, nz), 1)
     for j, (blk, g) in enumerate(((0, 3), (1, 0), (1, 1), (1, 2), (1, 3), (2, 0))):
-        table = jnp.where(rows_b == g * group + cols_b // 4, 1.0, 0.0).astype(jnp.bfloat16)
-        grown[j] = dot_exact(value[blk], table)
+        grown[j] = dot_exact(value[blk], back[g])
 
     for copy in round_2:
         copy.wait_recv()
@@ -358,8 +363,8 @@
     sweep(one, two, x0 - 1, x1 + 1)
 
     def emit_last(at, v, *terms):
-        up_out[at - x0] = v[0:ny]
-        res_out[at - x0] = residual_at(at, v, *terms)
+        up_out[at - x0] = 0.5 * v[0:ny]
+        res_out[at - x0] = 0.5 * residual_at(at, v, *terms)
 
     walk(two, x0, x1, emit_last)
     for copy in round_1 + coarse_c + coarse_s:
@@ -377,7 +382,7 @@
         half = pltpu.VMEM((nx // 2 + 4, 8, nz), F32)
         dma = pltpu.SemaphoreType.DMA
         shape = jax.ShapeDtypeStruct(potential.shape, F32)
-        return pl.pallas_call(
+        updated, residual = pl.pallas_call(
             functools.partial(kernel, gx_n, gy_n),
             out_shape=(shape, shape),
             in_specs=[pl.BlockSpec(memory_space=pl.ANY)] * 3,
@@ -393,6 +398,7 @@
                 pltpu.VMEM((8, nz), F32),
                 pltpu.VMEM((2, 6, 8, nz), F32), pltpu.VMEM((8, 3, 8, nz), F32), pltpu.VMEM((8, 8, nz), F32),
                 pltpu.VMEM((7, 3, 16, nz), F32), pltpu.VMEM((6, 16, nz), F32),
+                pltpu.VMEM((4, nz, nz), jnp.bfloat16),
                 dma((3,)), dma((12,)), dma((12,)), dma((8,)), dma((8,)),
                 dma((8,)), dma((8,)), dma((8,)), dma((8,)),
             ],
@@ -402,6 +408,7 @@
         )(*[
             pltpu.with_memory_space_constraint(v, pltpu.HBM) for v in (potential, density, correction)
         ])
+        return 2.0 * updated, 2.0 * residual
 
     placed = (P("gx", "gy", None),) * 3
     return jax.shard_map(

time: 24.3 us -> 22.2 us (0.914)
  Pallas kernels: 22.1 us -> 20.6 us
  local copies, waits for them, and re-layouts: 1.36 us -> 0 us
  other arithmetic: 0 us -> 0.77 us
    pallas_call x1, Pallas kernels: 22.1 us -> 20.6 us  [shards(): pl.pallas_call(functools.partial(kernel, gx_n, gy_n), out_shape=(shape, s...]
    unnamed x2 -> x0, local copies, waits for them, and re-layouts: 1.36 us -> none
    mul x0 -> x1, other arithmetic: none -> 0.77 us  [shards(): return (2.0 * updated, 2.0 * residual)]
where the time goes in v4:
time: 22.2 us; the launch traced here: 22 us
  Pallas kernels  20.6 us (93%)
  other arithmetic  0.77 us (3%)
  between operations  0.64 us (3%)
    pallas_call x1, Pallas kernels, shards(): pl.pallas_call(functools.partial(kernel, gx_n, gy_n), out_shape=(shape, s...  20.6 us
    mul x1, other arithmetic, shards(): return (2.0 * updated, 2.0 * residual)  0.77 us

profile of v4, /device:TPU:0, one launch (start us, length us, event | category | flops | bytes accessed | tf_op | source)
XLA Modules:
  0.0 22.0 jit_solution(10939966935463596216)
XLA Ops:
  0.6 20.6 %shard_map.50 = (f32[24,16,128]{2,1,0:T(8,128)S(1)}, f32[24,16,128]{2,1,0:T(8,128)S(1)}) custom-call(f32[24,16,128]{2,1,0:T(8,128)} %p_in.1, f32[24,16,128]{2,1,0:T(8,128)} %d_in.1, f32[24,16,128]{2,1,0:T(8,128)} %c_in.1), custom_call_target="tpu_custom_call" | custom-call | tf_op jit(solution)/shard_map/pallas_call | solution.py:385
  21.3 0.8 %broadcast_multiply_fusion = (f32[24,16,128]{2,1,0:T(8,128)}, f32[24,16,128]{2,1,0:T(8,128)}) fusion(f32[24,16,128]{2,1,0:T(8,128)S(1)} %get-tuple-element.5, f32[24,16,128]{2,1,0:T(8,128)S(1)} %get-tuple-element.4), kind=kLoop, calls=%fused_computation | loop fusion | flops 98304 | bytes 786432 | tf_op jit(solution)/shard_map/mul | solution.py:411

commit v5 on v4

--- a/solution.py
+++ b/solution.py
@@ -335,27 +335,31 @@
     for j, (blk, g) in enumerate(((0, 3), (1, 0), (1, 1), (1, 2), (1, 3), (2, 0))):
         grown[j] = dot_exact(value[blk], back[g])
 
+    def row(j, i):
+        return jnp.broadcast_to(grown[j, 3 + i : 4 + i, :], (8, nz))
+
+    def add_own_rows(i, base):
+        a0 = jnp.where(sub < 4, row(1, i), row(2, i))
+        a1 = jnp.where(sub < 4, row(3, i), row(4, i))
+        for at in range(max(4 * i, 1), min(4 * i + 4, x1 + 3)):
+            fin[at, 0:8] = base[at, 0:8] + a0
+            fin[at, 8:16] = base[at, 8:16] + a1
+
+    for i in range(1, nx // 4 + 1):
+        add_own_rows(i, two)
     for copy in round_2:
         copy.wait_recv()
-
-    def row(j, i):
-        return jnp.broadcast_to(grown[j, 3 + i : 4 + i, :], (8, nz))
-
+    add_own_rows(0, fin)
+    add_own_rows(nx // 4 + 1, fin)
     for i in range(nx // 4 + 2):
-        a0 = jnp.where(sub < 4, row(1, i), row(2, i))
-        a1 = jnp.where(sub < 4, row(3, i), row(4, i))
         a2 = jnp.where(sub < 4, row(5, i), row(0, i))
-        for at in range(4 * i, 4 * i + 4):
-            if 1 <= at < x1 + 3:
-                base = two if x0 <= at < x1 else fin
-                fin[at, 0:8] = base[at, 0:8] + a0
-                fin[at, 8:16] = base[at, 8:16] + a1
-                lo, hi = est_lo[at // 2], est_hi[at // 2]
-                if at % 2 == 0:
-                    lo = pltpu.roll(lo, 4, 0)
-                else:
-                    hi = pltpu.roll(hi, 4, 0)
-                fin[at, ny : ny + 8] = jnp.where(sub < 4, hi, lo) + a2
+        for at in range(max(4 * i, 1), min(4 * i + 4, x1 + 3)):
+            lo, hi = est_lo[at // 2], est_hi[at // 2]
+            if at % 2 == 0:
+                lo = pltpu.roll(lo, 4, 0)
+            else:
+                hi = pltpu.roll(hi, 4, 0)
+            fin[at, ny : ny + 8] = jnp.where(sub < 4, hi, lo) + a2
 
     sweep(fin, one, x0 - 2, x1 + 2)
     for copy in round_2:

time: 22.2 us -> 22.2 us (level)
  no operation moved by 1% of the time
where the time goes in v5:
time: 22.2 us; the launch traced here: 22 us
  Pallas kernels  20.6 us (93%)
  other arithmetic  0.77 us (3%)
  between operations  0.64 us (3%)
    pallas_call x1, Pallas kernels, shards(): pl.pallas_call(functools.partial(kernel, gx_n, gy_n), out_shape=(shape, s...  20.6 us
    mul x1, other arithmetic, shards(): return (2.0 * updated, 2.0 * residual)  0.77 us

profile of v5, /device:TPU:0, one launch (start us, length us, event | category | flops | bytes accessed | tf_op | source)
XLA Modules:
  0.0 22.0 jit_solution(4861131728637753443)
XLA Ops:
  0.6 20.6 %shard_map.50 = (f32[24,16,128]{2,1,0:T(8,128)S(1)}, f32[24,16,128]{2,1,0:T(8,128)S(1)}) custom-call(f32[24,16,128]{2,1,0:T(8,128)} %p_in.1, f32[24,16,128]{2,1,0:T(8,128)} %d_in.1, f32[24,16,128]{2,1,0:T(8,128)} %c_in.1), custom_call_target="tpu_custom_call" | custom-call | tf_op jit(solution)/shard_map/pallas_call | solution.py:389
  21.3 0.8 %broadcast_multiply_fusion = (f32[24,16,128]{2,1,0:T(8,128)}, f32[24,16,128]{2,1,0:T(8,128)}) fusion(f32[24,16,128]{2,1,0:T(8,128)S(1)} %get-tuple-element.5, f32[24,16,128]{2,1,0:T(8,128)S(1)} %get-tuple-element.4), kind=kLoop, calls=%fused_computation | loop fusion | flops 98304 | bytes 786432 | tf_op jit(solution)/shard_map/mul | solution.py:415
